TPU v7x, 256 devices: a whole 4x4x8 slice. The times are simulated.
256 devices in a mesh: query: 8 (over x_hi, y), corpus: 32 (over z, x_lo, core).
Axes of the slice: x: 4 (x_hi: 2, x_lo: 2; x = x_hi * 2 + x_lo), y: 4, z: 8, core: 2. Of those that a mesh axis runs over, the one named last changes fastest.
Arguments:
- queries: float32 [3072, 768], P('query'), may hold values from -20 to 20
- codes: int32 [32768, 96], P('corpus'), may hold values from 0 to 255
- positive: int32 [3072], P('query'), may hold values from 0 to 32767
- codebook: float32 [256, 768], replicated, may hold values from -0.6 to 0.6
Outputs:
- grad_queries: float32 [3072, 768], P('query')
- grad_codebook: float32 [256, 768], replicated
- loss: float32 [3072], P('query')
All inputs are finite; a program needn't handle non-finite values.
Results may differ from a plain program's by a relative error of at most 0.0003.
Values sent between devices are 32-bit elements; how exact they have to be, the bound alone decides.
A program may use at most 64 MiB of HBM per device.

v0:
```python
import jax
import jax.numpy as jnp
from jax import lax
from jax.experimental import pallas as pl
from jax.experimental.pallas import tpu as pltpu
from jax.sharding import PartitionSpec as P

F32, BF16, I32 = jnp.float32, jnp.bfloat16, jnp.int32
NN = (((1,), (0,)), ((), ()))
NT = (((1,), (1,)), ((), ()))
HIGH_CODES = 64
LOW_CODES = 4


def dot(a, b, dims=NN):
    return lax.dot_general(a, b, dims, preferred_element_type=F32)


def split(x):
    high = x.astype(BF16)
    return high, (x - high.astype(F32)).astype(BF16)


def split3(x):
    high = x.astype(BF16)
    rest = x - high.astype(F32)
    mid = rest.astype(BF16)
    return high, mid, (rest - mid.astype(F32)).astype(BF16)


def transpose_inputs(codes_ref, book_ref, codes_t, book_t):
    codes_t[...] = codes_ref[...].T
    book_t[...] = book_ref[...].T


def split_queries(q_ref, q3, q_t):
    width = q_ref.shape[1]
    high, mid, low = split3(q_ref[...])
    q3[:, :width] = high
    q3[:, width : 2 * width] = mid
    q3[:, 2 * width :] = low
    rows = q_ref.shape[0]
    high, mid = split(q_ref[...].T)
    q_t[:, :rows] = high
    q_t[:, rows:] = mid


def rebuild(codes_t, book_t, r3):
    subs, docs = codes_t.shape
    width = book_t.shape[0]
    sub_width = width // subs

    def pair(p, _):
        parts = []
        for side in range(2):
            m = 2 * p + side
            base = pl.multiple_of(m * sub_width, sub_width)
            low = book_t[pl.ds(base, sub_width), :128]
            high = book_t[pl.ds(base, sub_width), 128:]
            code = codes_t[pl.ds(m, 1), :]
            tiles = []
            for t in range(docs // 128):
                picked = jnp.broadcast_to(code[:, 128 * t : 128 * t + 128], (sub_width, 128))
                lane = picked & 127
                a = jnp.take_along_axis(low, lane, axis=1)
                b = jnp.take_along_axis(high, lane, axis=1)
                tiles.append(jnp.where(picked < 128, a, b))
            parts.append(jnp.concatenate(tiles, axis=1))
        both = jnp.concatenate(parts, axis=0)
        high, mid, low = split3(both)
        at = pl.multiple_of(2 * p * sub_width, 2 * sub_width)
        r3[pl.ds(at, 2 * sub_width), :] = low
        r3[pl.ds(width + at, 2 * sub_width), :] = mid
        r3[pl.ds(2 * width + at, 2 * sub_width), :] = high
        return 0

    lax.fori_loop(0, subs // 2, pair, 0)


def score(q3, r3, s_ref, tile=256):
    width = q3.shape[1] // 3

    def block(t, _):
        at = pl.ds(pl.multiple_of(t * tile, tile), tile)
        acc = dot(q3[...], r3[:, at])
        acc = acc + dot(q3[:, : 2 * width], r3[width:, at])
        acc = acc + dot(q3[:, :width], r3[2 * width :, at])
        s_ref[:, at] = acc
        return 0

    lax.fori_loop(0, s_ref.shape[1] // tile, block, 0)


def statistics(s_ref, pos_col, cols, step=32):
    rows, docs = s_ref.shape
    lane = lax.broadcasted_iota(I32, (step, 128), 1)
    ids = lax.broadcasted_iota(I32, (step, docs), 1)

    def block(b, _):
        at = pl.ds(pl.multiple_of(b * step, step), step)
        s = s_ref[at, :]
        top = jnp.max(s, axis=1, keepdims=True)
        own = jnp.sum(jnp.where(pos_col[at, :1] == ids, s, 0.0), axis=1, keepdims=True)
        e = jnp.exp(s - top)
        total = jnp.sum(e, axis=1, keepdims=True)
        s_ref[at, :] = e
        cols[at, :] = jnp.where(
            lane == 0, top, jnp.where(lane == 1, total, jnp.where(lane == 2, own, 0.0))
        )
        return 0

    lax.fori_loop(0, rows // step, block, 0)


def as_column(row, column):
    column[...] = jnp.broadcast_to(row, (128, row.shape[1])).T


def weigh(e_ref, scale_col, pos_col, w2, step=32):
    rows, docs = e_ref.shape
    ids = lax.broadcasted_iota(I32, (step, docs), 1)

    def block(b, _):
        at = pl.ds(pl.multiple_of(b * step, step), step)
        w = e_ref[at, :] * scale_col[at, :1]
        w = w - jnp.where(pos_col[at, :1] == ids, 1.0, 0.0)
        high, low = split(w)
        w2[at, :] = low
        w2[pl.ds(pl.multiple_of(rows + b * step, step), step), :] = high
        return 0

    lax.fori_loop(0, rows // step, block, 0)


def query_gradient(w2, r3, out, tile=256):
    rows = w2.shape[0] // 2
    width = r3.shape[0] // 3

    def block(t, _):
        base = pl.multiple_of(t * tile, tile)
        mid = r3[pl.ds(width + base, tile), :]
        high = r3[pl.ds(2 * width + base, tile), :]
        acc = dot(w2[rows:, :], mid, NT)
        acc = acc + dot(w2[:rows, :], high, NT)
        acc = acc + dot(w2[rows:, :], high, NT)
        out[:, pl.ds(base, tile)] = acc
        return 0

    lax.fori_loop(0, width // tile, block, 0)


def document_gradient(w2, q_t, out, tile=256):
    rows = w2.shape[0] // 2

    def block(t, _):
        at = pl.ds(pl.multiple_of(t * tile, tile), tile)
        acc = dot(q_t[...], w2[:, at])
        out[:, at] = acc + dot(q_t[:, :rows], w2[rows:, at])
        return 0

    lax.fori_loop(0, out.shape[1] // tile, block, 0)


def collect(codes_t, d_ref, out, group=4):
    subs, docs = codes_t.shape
    sub_width = d_ref.shape[0] // subs
    word = lax.broadcasted_iota(I32, (HIGH_CODES, docs), 0)
    lane = lax.broadcasted_iota(I32, (sub_width, 128), 1)

    def block(g, _):
        tables, values = [], []
        for s in range(group):
            m = group * g + s
            code = codes_t[pl.ds(m, 1), :]
            inner = code & (HIGH_CODES - 1)
            outer = jnp.broadcast_to(code >> 6, (sub_width, docs))
            tables.append(jnp.where(word == inner, 1.0, 0.0).astype(BF16))
            d = d_ref[pl.ds(pl.multiple_of(m * sub_width, sub_width), sub_width), :]
            high = d.astype(BF16).astype(F32)
            low = d - high
            masks = [outer == k for k in range(LOW_CODES)]
            rows = [jnp.where(mask, part, 0.0) for part in (high, low) for mask in masks]
            values.append(jnp.concatenate(rows, axis=0).astype(BF16))
        found = dot(jnp.concatenate(values, axis=0), jnp.concatenate(tables, axis=0), NT)
        rows = 2 * LOW_CODES * sub_width
        for s in range(group):
            at = 128 * (s // 2)
            piece = found[rows * s : rows * (s + 1), at : at + 128]
            piece = piece[: rows // 2] + piece[rows // 2 :]
            parts = [piece[sub_width * k : sub_width * (k + 1)] for k in range(LOW_CODES)]
            base = pl.multiple_of((group * g + s) * sub_width, sub_width)
            for k in range(2):
                first, second = parts[2 * k], parts[2 * k + 1]
                if s % 2:
                    first = pltpu.roll(first, 64, 1)
                else:
                    second = pltpu.roll(second, 64, 1)
                out[pl.ds(base, sub_width), 128 * k : 128 * k + 128] = jnp.where(
                    lane < 64, first, second
                )
        return 0

    lax.fori_loop(0, subs // group, block, 0)


def front(q_ref, codes_ref, pos_ref, book_ref, r3, q_t, codes_t, e_ref, stats, book_t, q3, pos_col, cols):
    transpose_inputs(codes_ref, book_ref, codes_t, book_t)
    split_queries(q_ref, q3, q_t)
    rebuild(codes_t, book_t, r3)
    score(q3, r3, e_ref)
    as_column(pos_ref[...], pos_col)
    statistics(e_ref, pos_col, cols)
    stats[...] = cols[...].T[:8]


def back(r3, q_t, codes_t, e_ref, pos_ref, scale_ref, grad_q, grad_b, pos_col, scale_col, w2, d_ref):
    as_column(pos_ref[...], pos_col)
    as_column(scale_ref[...], scale_col)
    weigh(e_ref, scale_col, pos_col, w2)
    query_gradient(w2, r3, grad_q)
    document_gradient(w2, q_t, d_ref)
    collect(codes_t, d_ref, grad_b)


def local(queries, codes, positive, codebook):
    rows, width = queries.shape
    docs, subs = codes.shape
    words = codebook.shape[0]
    here = (positive - lax.axis_index("corpus") * docs).reshape(1, rows)
    r3, q_t, codes_t, e, stats = pl.pallas_call(
        front,
        out_shape=(
            jax.ShapeDtypeStruct((3 * width, docs), BF16),
            jax.ShapeDtypeStruct((width, 2 * rows), BF16),
            jax.ShapeDtypeStruct((subs, docs), I32),
            jax.ShapeDtypeStruct((rows, docs), F32),
            jax.ShapeDtypeStruct((8, rows), F32),
        ),
        scratch_shapes=[
            pltpu.VMEM((width, words), F32),
            pltpu.VMEM((rows, 3 * width), BF16),
            pltpu.VMEM((rows, 128), I32),
            pltpu.VMEM((rows, 128), F32),
        ],
        name="front",
    )(queries, codes, here, codebook)
    every = lax.all_gather(stats, "corpus")
    row_top = jnp.max(every[:, 0], axis=0)
    row_total = jnp.sum(every[:, 1] * jnp.exp(every[:, 0] - row_top), axis=0)
    log_total = row_top + jnp.log(row_total)
    loss = log_total - jnp.sum(every[:, 2], axis=0)
    scale = jnp.exp(stats[0] - log_total).reshape(1, rows)
    grad_q, grad_b = pl.pallas_call(
        back,
        out_shape=(
            jax.ShapeDtypeStruct((rows, width), F32),
            jax.ShapeDtypeStruct((width, words), F32),
        ),
        scratch_shapes=[
            pltpu.VMEM((rows, 128), I32),
            pltpu.VMEM((rows, 128), F32),
            pltpu.VMEM((2 * rows, docs), BF16),
            pltpu.VMEM((width, docs), F32),
        ],
        name="back",
    )(r3, q_t, codes_t, e, here, scale)
    grad_q = lax.psum(grad_q, "corpus")
    grad_b = lax.psum(grad_b, ("query", "corpus"))
    return grad_q, grad_b.T, loss


def solution(mesh):
    return jax.shard_map(
        local,
        mesh=mesh,
        in_specs=(P("query", None), P("corpus", None), P("query"), P()),
        out_specs=(P("query", None), P(), P("query")),
        check_vma=False,
    )
```

profile of v0, /device:TPU:1, one launch (start us, length us, event | category | flops | bytes accessed | tf_op | source)
XLA Modules:
  0.0 582.8 jit_solution(2827089352546931112)
XLA Ops:
  7.2 0.0 all-reduce.5.cloned.1.call-start
  7.2 0.7 broadcast_subtract_fusion
  7.9 0.6 reshape.27.pos_ref
  8.5 2.0 copy.7.codes_ref
  10.5 20.3 %front.1 = (bf16[2304,1024]{1,0:T(8,128)(2,1)}, bf16[768,768]{1,0:T(8,128)(2,1)}, s32[96,1024]{1,0:T(8,128)}, f32[384,1024]{1,0:T(8,128)}, f32[8,384]{1,0:T(8,128)}) custom-call(f32[384,768]{1,0:T(8,128)} %q_ref.1, s32[1024,96]{1,0:T(8,128)} %copy.7.codes_ref, s32[1,384]{1,0:T(1,128)} %reshape.27.pos_ref, f32[256,768]{1,0:T(8,128)} %book_ref.1), custom_call_target="tpu_custom_call" | custom-call | tf_op jit(solution)/shard_map/front/pallas_call | solution.py:230
  30.8 39.8 %all-gather = f32[256,384]{1,0:T(8,128)S(1)} all-gather(f32[8,384]{1,0:T(8,128)} %get-tuple-element.14), channel_id=2, replica_groups=mesh['query'=8,'corpus'=32] {'corpus'}, dimensions={0}, use_global_device_ids=true | all-gather | bytes 405504 | tf_op jit(solution)/shard_map/all_gather | solution.py:247
  70.6 0.1 slice_reduce_fusion
  70.8 0.6 fusion.4
  71.3 1.3 subtract_exponential_fusion.scale_ref
  72.6 20.7 %back.1 = (f32[384,768]{1,0:T(8,128)}, f32[768,256]{1,0:T(8,128)}) custom-call(bf16[2304,1024]{1,0:T(8,128)(2,1)} %get-tuple-element.10.r3, bf16[768,768]{1,0:T(8,128)(2,1)} %get-tuple-element.11.q_t, s32[96,1024]{1,0:T(8,128)} %get-tuple-element.12.codes_t, f32[384,1024]{1,0:T(8,128)} %get-tuple-element.13.e_ref, s32[1,384]{1,0:T(1,128)} %reshape.27.pos_ref, ...), custom_call_target="tpu_custom_call" | custom-call | tf_op jit(solution)/shard_map/back/pallas_call | solution.py:253
  93.4 0.0 all-reduce.5.cloned.1.call-update
  93.4 0.0 all-reduce.3.cloned.1.call-start
  93.5 0.7 all-reduce.3.cloned.1.call-update
  94.2 251.9 %all-reduce.5.cloned.1.call-done = f32[256,768]{0,1:T(8,128)} async-done(((f32[256,768]{0,1:T(8,128)}), f32[256,768]{0,1:T(8,128)}) %all-reduce.5.cloned.1.call-update) | async-done | bytes 786448 | tf_op jit(solution)/shard_map/psum | solution.py:268
  346.1 2.3 copy.9
  348.4 225.2 %all-reduce.3.cloned.1.call-done = f32[384,768]{1,0:T(8,128)} async-done(((f32[384,768]{1,0:T(8,128)}), f32[384,768]{1,0:T(8,128)}) %all-reduce.3.cloned.1.call-update) | async-done | bytes 1179664 | tf_op jit(solution)/shard_map/psum | solution.py:267
  573.6 2.4 copy.25
  (1 shorter events, 0.0 us)
Async XLA Ops:
  7.2 338.9 %all-reduce.5.cloned.1.call-start = ((), (), s32[]{:S(2)}) async-start(), calls=%async_computation.1 | async-start | bytes 1572864 | tf_op jit(solution)/shard_map/psum | solution.py:268
  93.4 480.2 %all-reduce.3.cloned.1.call-start = ((), (), s32[]{:S(2)}) async-start(), calls=%async_computation | async-start | bytes 2359296 | tf_op jit(solution)/shard_map/psum | solution.py:267
Sparse Core Ops, SparseCore 0:
  93.5 252.5 all-reduce.4
  348.7 224.7 all-reduce.2
where the time goes:
time: 583 us
  waiting for transfers between devices  478 us (82%)
  Pallas kernels  41.1 us (7%)
  blocking collectives  39.8 us (7%)
  between operations  14 us (2%)
  local copies, waits for them, and re-layouts  7.2 us (1%)
    psum x1, waiting for transfers between devices, local(): grad_b = lax.psum(grad_b, ('query', 'corpus'))  252 us
    psum x1, waiting for transfers between devices, local(): grad_q = lax.psum(grad_q, 'corpus')  225 us
    all_gather x1, blocking collectives, local(): every = lax.all_gather(stats, 'corpus')  39.8 us
    pallas_call x1, Pallas kernels, local(): pl.pallas_call(back, out_shape=(jax.ShapeDtypeStruct((rows, width), F32),...  20.7 us
    pallas_call x1, Pallas kernels, local(): pl.pallas_call(front, out_shape=(jax.ShapeDtypeStruct((3 * width, docs),...  20.3 us
  transfers between devices with their start and end apart: 2, of which 2 were waited for; matrix products, arithmetic and copies ran while one was open for 0% of the time, Pallas kernels for 0%

commit v1 on v0

--- a/solution.py
+++ b/solution.py
@@ -26,11 +26,6 @@
     rest = x - high.astype(F32)
     mid = rest.astype(BF16)
     return high, mid, (rest - mid.astype(F32)).astype(BF16)
-
-
-def transpose_inputs(codes_ref, book_ref, codes_t, book_t):
-    codes_t[...] = codes_ref[...].T
-    book_t[...] = book_ref[...].T
 
 
 def split_queries(q_ref, q3, q_t):
@@ -161,13 +156,14 @@
     lax.fori_loop(0, out.shape[1] // tile, block, 0)
 
 
-def collect(codes_t, d_ref, out, group=4):
+def collect(codes_t, d_ref, out, blocks, base, group=4):
     subs, docs = codes_t.shape
     sub_width = d_ref.shape[0] // subs
     word = lax.broadcasted_iota(I32, (HIGH_CODES, docs), 0)
     lane = lax.broadcasted_iota(I32, (sub_width, 128), 1)
 
-    def block(g, _):
+    def block(b, _):
+        g = lax.rem(b + base, subs // group)
         tables, values = [], []
         for s in range(group):
             m = group * g + s
@@ -188,23 +184,23 @@
             piece = found[rows * s : rows * (s + 1), at : at + 128]
             piece = piece[: rows // 2] + piece[rows // 2 :]
             parts = [piece[sub_width * k : sub_width * (k + 1)] for k in range(LOW_CODES)]
-            base = pl.multiple_of((group * g + s) * sub_width, sub_width)
+            start = pl.multiple_of((group * g + s) * sub_width, sub_width)
             for k in range(2):
                 first, second = parts[2 * k], parts[2 * k + 1]
                 if s % 2:
                     first = pltpu.roll(first, 64, 1)
                 else:
                     second = pltpu.roll(second, 64, 1)
-                out[pl.ds(base, sub_width), 128 * k : 128 * k + 128] = jnp.where(
+                out[pl.ds(start, sub_width), 128 * k : 128 * k + 128] = jnp.where(
                     lane < 64, first, second
                 )
         return 0
 
-    lax.fori_loop(0, subs // group, block, 0)
-
-
-def front(q_ref, codes_ref, pos_ref, book_ref, r3, q_t, codes_t, e_ref, stats, book_t, q3, pos_col, cols):
-    transpose_inputs(codes_ref, book_ref, codes_t, book_t)
+    lax.fori_loop(blocks[0], blocks[1], block, 0)
+
+
+def front(q_ref, codes_t, pos_ref, book_ref, r3, q_t, e_ref, stats, book_t, q3, pos_col, cols):
+    book_t[...] = book_ref[...].T
     split_queries(q_ref, q3, q_t)
     rebuild(codes_t, book_t, r3)
     score(q3, r3, e_ref)
@@ -213,13 +209,261 @@
     stats[...] = cols[...].T[:8]
 
 
-def back(r3, q_t, codes_t, e_ref, pos_ref, scale_ref, grad_q, grad_b, pos_col, scale_col, w2, d_ref):
+class Place:
+    def __init__(self):
+        query, corpus = lax.axis_index("query"), lax.axis_index("corpus")
+        self.y = lax.rem(query, 4)
+        self.x = 2 * lax.div(query, 4) + lax.rem(lax.div(corpus, 2), 2)
+        self.z = lax.div(corpus, 4)
+        self.core = lax.rem(corpus, 2)
+
+    def at(self, x=None, y=None, z=None, core=None):
+        x = self.x if x is None else x
+        y = self.y if y is None else y
+        z = self.z if z is None else z
+        core = self.core if core is None else core
+        return (4 * lax.div(x, 2) + y, 4 * z + 2 * lax.rem(x, 2) + core)
+
+    def next_y(self, d):
+        return lax.rem(self.y + d, 4)
+
+    def next_x(self, d):
+        return lax.rem(self.x + d, 4)
+
+    def next_z(self, d):
+        return lax.rem(self.z + d, 8)
+
+
+class Wire:
+    def __init__(self, sent, arrived):
+        self.sent, self.arrived, self.copies = sent, arrived, []
+
+    def send(self, src, dst, device):
+        i = len(self.copies)
+        copy = pltpu.make_async_remote_copy(
+            src_ref=src,
+            dst_ref=dst,
+            send_sem=self.sent.at[i],
+            recv_sem=self.arrived.at[i],
+            device_id=device,
+            device_id_type=pl.DeviceIdType.MESH,
+        )
+        copy.start()
+        self.copies.append(copy)
+        return copy
+
+    def finish(self):
+        for copy in self.copies:
+            copy.wait_send()
+
+
+def rows_at(index, size):
+    return pl.ds(pl.multiple_of(index * size, size), size)
+
+
+def merge(stats):
+    top = stats[0][0:1]
+    for s in stats[1:]:
+        top = jnp.maximum(top, s[0:1])
+    total = sum(s[1:2] * jnp.exp(s[0:1] - top) for s in stats)
+    own = sum(s[2:3] for s in stats)
+    pad = jnp.zeros((8 - 3, top.shape[1]), F32)
+    return jnp.concatenate([top, total, own, pad], axis=0)
+
+
+def back(
+    r3, q_t, codes_t, e_ref, pos_ref, stats_ref,
+    grad_q, grad_b, loss_ref,
+    pos_col, scale_col, w2, d_ref,
+    near, far, part_q, half_q, sum_q, up, down, cross,
+    part_b, half_b, sum_b, first_in, first_sum, second_in, second_sum, last_in,
+    sent, arrived,
+):
+    me = Place()
+    wire = Wire(sent, arrived)
+    x_pair = me.x + 1 - 2 * lax.rem(me.x, 2)
+    other = 1 - me.core
+    partners = [me.at(core=other), me.at(x=x_pair), me.at(x=x_pair, core=other)]
+    far_partners = [me.at(z=me.next_z(d)) for d in range(1, 8)]
+    y_partners = [me.at(y=me.next_y(d)) for d in range(1, 4)]
+    x_partners = [me.at(x=me.next_x(d)) for d in range(1, 4)]
+    greeted = [partners[0], partners[2]] + far_partners + y_partners + x_partners
+    barrier = pltpu.get_barrier_semaphore()
+    for device in greeted:
+        pl.semaphore_signal(barrier, inc=1, device_id=device, device_id_type=pl.DeviceIdType.MESH)
     as_column(pos_ref[...], pos_col)
-    as_column(scale_ref[...], scale_col)
+    pl.semaphore_wait(barrier, len(greeted))
+
+    mine = 2 * lax.rem(me.x, 2) + me.core
+    near[mine] = stats_ref[...]
+    copies = [wire.send(stats_ref, near.at[mine], device) for device in partners]
+    for copy in copies:
+        copy.wait_recv()
+    far[me.z] = merge([near[k] for k in range(4)])
+    copies = [wire.send(far.at[me.z], far.at[me.z], device) for device in far_partners]
+    for copy in copies:
+        copy.wait_recv()
+    whole = merge([far[k] for k in range(8)])
+    log_total = whole[0:1] + jnp.log(whole[1:2])
+    loss_ref[...] = log_total - whole[2:3]
+    as_column(jnp.exp(stats_ref[0:1] - log_total), scale_col)
+
     weigh(e_ref, scale_col, pos_col, w2)
-    query_gradient(w2, r3, grad_q)
+    query_gradient(w2, r3, part_q)
+    half = part_q.shape[0] // 2
+    chunk = half // 8
+    q_core = wire.send(part_q.at[rows_at(other, half)], half_q, partners[0])
     document_gradient(w2, q_t, d_ref)
-    collect(codes_t, d_ref, grad_b)
+    q_core.wait_recv()
+    sum_q[...] = part_q[rows_at(me.core, half)] + half_q[...]
+
+    z_up, z_down = far_partners[0], far_partners[6]
+
+    def ring_send(step):
+        copies = []
+        for buffers, ahead, steps, device in ((up, 4 - step, 4, z_up), (down, 8 - 3 + step, 3, z_down)):
+            if step >= steps:
+                continue
+            at = rows_at(me.next_z(ahead), chunk)
+            if step == 0:
+                src = sum_q.at[at]
+            else:
+                src = buffers.at[step - 1]
+                src[...] = src[...] + sum_q[at]
+            copies.append(wire.send(src, buffers.at[step], device))
+        return copies
+
+    def arrive(copies):
+        for copy in copies:
+            copy.wait_recv()
+
+    subs = codes_t.shape[0]
+    groups = subs // 4
+    base = other * (groups // 2)
+    b_half = part_b.shape[0] // 2
+
+    copies = ring_send(0)
+    collect(codes_t, d_ref, part_b, (0, groups // 4), base)
+    arrive(copies)
+    copies = ring_send(1)
+    collect(codes_t, d_ref, part_b, (groups // 4, groups // 2), base)
+    b_core = wire.send(part_b.at[rows_at(other, b_half)], half_b, partners[0])
+    arrive(copies)
+    copies = ring_send(2)
+    collect(codes_t, d_ref, part_b, (groups // 2, 3 * groups // 4), base)
+    arrive(copies)
+    copies = ring_send(3)
+    collect(codes_t, d_ref, part_b, (3 * groups // 4, groups), base)
+    b_core.wait_recv()
+    sum_b[...] = part_b[rows_at(me.core, b_half)] + half_b[...]
+
+    lines = b_half // 4
+    order = (
+        ((me.y, me.next_y, y_partners), (me.x, me.next_x, x_partners)),
+        ((me.x, me.next_x, x_partners), (me.y, me.next_y, y_partners)),
+    )
+    firsts = []
+    for k in range(2):
+        columns = pl.ds(128 * k, 128)
+        _, following, devices = order[k][0]
+        for d in range(1, 4):
+            firsts.append(
+                wire.send(
+                    sum_b.at[rows_at(following(d), lines), columns],
+                    first_in.at[k, d - 1],
+                    devices[d - 1],
+                )
+            )
+
+    arrive(copies)
+    own = sum_q[rows_at(me.z, chunk)] + (up[3] + down[2])
+    cross[0] = own
+    across = wire.send(cross.at[0], cross.at[1], partners[1])
+
+    seconds = []
+    arrive(firsts)
+    for k in range(2):
+        index, _, _ = order[k][0]
+        columns = pl.ds(128 * k, 128)
+        acc = sum_b[rows_at(index, lines), columns]
+        for d in range(3):
+            acc = acc + first_in[k, d]
+        first_sum[k] = acc
+        _, following, devices = order[k][1]
+        for d in range(1, 4):
+            seconds.append(
+                wire.send(
+                    first_sum.at[k, rows_at(following(d), lines // 4)],
+                    second_in.at[k, d - 1],
+                    devices[d - 1],
+                )
+            )
+
+    def q_rows(z):
+        return pl.ds(pl.multiple_of(me.core * half + z * chunk, chunk), chunk)
+
+    arrive([across])
+    grad_q[q_rows(me.z)] = cross[0] + cross[1]
+    passed = [wire.send(grad_q.at[q_rows(me.z)], grad_q.at[q_rows(me.z)], partners[0])]
+
+    def pass_on(step):
+        copies = []
+        for back_by, steps, device in ((8 - step, 4, z_up), (step, 3, z_down)):
+            if step < steps:
+                at = q_rows(me.next_z(back_by))
+                copies.append(wire.send(grad_q.at[at], grad_q.at[at], device))
+        return copies
+
+    def to_core(step):
+        for ahead, steps in ((8 - step - 1, 4), (step + 1, 3)):
+            if step < steps:
+                at = q_rows(me.next_z(ahead))
+                passed.append(wire.send(grad_q.at[at], grad_q.at[at], partners[0]))
+
+    copies = pass_on(0)
+
+    arrive(seconds)
+    for k in range(2):
+        index, _, _ = order[k][1]
+        acc = first_sum[k, rows_at(index, lines // 4)]
+        for d in range(3):
+            acc = acc + second_in[k, d]
+        last_in[me.z, k] = acc
+    lasts = [wire.send(last_in.at[me.z], last_in.at[me.z], device) for device in far_partners]
+
+    for step in range(3):
+        arrive(copies)
+        copies = pass_on(step + 1)
+        to_core(step)
+        if step == 1:
+            arrive(lasts)
+            acc = last_in[0]
+            for z in range(1, 8):
+                acc = acc + last_in[z]
+            seconds = []
+            for k in range(2):
+                columns = pl.ds(128 * k, 128)
+                at = me.core * b_half + order[k][0][0] * lines + order[k][1][0] * (lines // 4)
+                at = pl.ds(pl.multiple_of(at, lines // 4), lines // 4)
+                grad_b[at, columns] = acc[k]
+                for device in order[k][1][2]:
+                    seconds.append(wire.send(grad_b.at[at, columns], grad_b.at[at, columns], device))
+        if step == 2:
+            arrive(seconds)
+            firsts = []
+            for k in range(2):
+                columns = pl.ds(128 * k, 128)
+                at = me.core * b_half + order[k][0][0] * lines
+                at = pl.ds(pl.multiple_of(at, lines), lines)
+                for device in order[k][0][2]:
+                    firsts.append(wire.send(grad_b.at[at, columns], grad_b.at[at, columns], device))
+    arrive(copies)
+    to_core(3)
+    arrive(firsts)
+    at = rows_at(me.core, b_half)
+    passed.append(wire.send(grad_b.at[at], grad_b.at[at], partners[0]))
+    arrive(passed)
+    wire.finish()
 
 
 def local(queries, codes, positive, codebook):
@@ -227,12 +471,12 @@
     docs, subs = codes.shape
     words = codebook.shape[0]
     here = (positive - lax.axis_index("corpus") * docs).reshape(1, rows)
-    r3, q_t, codes_t, e, stats = pl.pallas_call(
+    codes_t = codes.T
+    r3, q_t, e, stats = pl.pallas_call(
         front,
         out_shape=(
             jax.ShapeDtypeStruct((3 * width, docs), BF16),
             jax.ShapeDtypeStruct((width, 2 * rows), BF16),
-            jax.ShapeDtypeStruct((subs, docs), I32),
             jax.ShapeDtypeStruct((rows, docs), F32),
             jax.ShapeDtypeStruct((8, rows), F32),
         ),
@@ -243,30 +487,47 @@
             pltpu.VMEM((rows, 128), F32),
         ],
         name="front",
-    )(queries, codes, here, codebook)
-    every = lax.all_gather(stats, "corpus")
-    row_top = jnp.max(every[:, 0], axis=0)
-    row_total = jnp.sum(every[:, 1] * jnp.exp(every[:, 0] - row_top), axis=0)
-    log_total = row_top + jnp.log(row_total)
-    loss = log_total - jnp.sum(every[:, 2], axis=0)
-    scale = jnp.exp(stats[0] - log_total).reshape(1, rows)
-    grad_q, grad_b = pl.pallas_call(
+    )(queries, codes_t, here, codebook)
+    chunk = rows // 16
+    lines = width // 8
+    vmem = pl.BlockSpec(memory_space=pltpu.VMEM)
+    grad_q, grad_b, loss = pl.pallas_call(
         back,
+        in_specs=[vmem] * 6,
+        out_specs=(vmem, vmem, vmem),
         out_shape=(
             jax.ShapeDtypeStruct((rows, width), F32),
             jax.ShapeDtypeStruct((width, words), F32),
+            jax.ShapeDtypeStruct((1, rows), F32),
         ),
         scratch_shapes=[
             pltpu.VMEM((rows, 128), I32),
             pltpu.VMEM((rows, 128), F32),
             pltpu.VMEM((2 * rows, docs), BF16),
             pltpu.VMEM((width, docs), F32),
+            pltpu.VMEM((4, 8, rows), F32),
+            pltpu.VMEM((8, 8, rows), F32),
+            pltpu.VMEM((rows, width), F32),
+            pltpu.VMEM((rows // 2, width), F32),
+            pltpu.VMEM((rows // 2, width), F32),
+            pltpu.VMEM((4, chunk, width), F32),
+            pltpu.VMEM((3, chunk, width), F32),
+            pltpu.VMEM((2, chunk, width), F32),
+            pltpu.VMEM((width, words), F32),
+            pltpu.VMEM((width // 2, words), F32),
+            pltpu.VMEM((width // 2, words), F32),
+            pltpu.VMEM((2, 3, lines, words // 2), F32),
+            pltpu.VMEM((2, lines, words // 2), F32),
+            pltpu.VMEM((2, 3, lines // 4, words // 2), F32),
+            pltpu.VMEM((2, lines // 4, words // 2), F32),
+            pltpu.VMEM((8, 2, lines // 4, words // 2), F32),
+            pltpu.SemaphoreType.DMA((80,)),
+            pltpu.SemaphoreType.DMA((80,)),
         ],
+        compiler_params=pltpu.CompilerParams(collective_id=0, has_side_effects=True),
         name="back",
-    )(r3, q_t, codes_t, e, here, scale)
-    grad_q = lax.psum(grad_q, "corpus")
-    grad_b = lax.psum(grad_b, ("query", "corpus"))
-    return grad_q, grad_b.T, loss
+    )(r3, q_t, codes_t, e, here, stats)
+    return grad_q, grad_b.T, loss.reshape(rows)
 
 
 def solution(mesh):

time: 583 us -> 97.3 us (0.17)
  waiting for transfers between devices: 478 us -> 0 us
  Pallas kernels: 41.1 us -> 91.2 us
  blocking collectives: 39.8 us -> 0 us
  between operations: 14 us -> 0.66 us
    psum x2 -> x0, waiting for transfers between devices: 477 us -> none  [the longest x1 252 us: local(): grad_b = lax.psum(grad_b, ('query', 'corpus'))]
    pallas_call x1, Pallas kernels: 20.7 us -> 71.2 us  [local(): pl.pallas_call(back, in_specs=[vmem] * 6, out_specs=(vmem, vmem, vmem), o...]
    all_gather x1 -> x0, blocking collectives: 39.8 us -> none  [local(): every = lax.all_gather(stats, 'corpus')]
  transfers between devices with their start and end apart: 2 -> 0, of which waited for: 2 -> 0; matrix products, arithmetic and copies ran while one was open for 0% -> 0% of each run, Pallas kernels for 0% -> 0%
where the time goes in v1:
time: 97.3 us; the launch traced here: 97.1 us
  Pallas kernels  91.2 us (94%)
  local copies, waits for them, and re-layouts  3.96 us (4%)
  other arithmetic  1.28 us (1%)
    pallas_call x1, Pallas kernels, local(): pl.pallas_call(back, in_specs=[vmem] * 6, out_specs=(vmem, vmem, vmem), o...  71.2 us
    pallas_call x1, Pallas kernels, local(): pl.pallas_call(front, out_shape=(jax.ShapeDtypeStruct((3 * width, docs),...  20.1 us
    unnamed x6, local copies, waits for them, and re-layouts  3.4 us

profile of v1, /device:TPU:1, one launch (start us, length us, event | category | flops | bytes accessed | tf_op | source)
XLA Modules:
  0.0 97.1 jit_solution(7856106637586322143)
XLA Ops:
  0.6 0.7 broadcast_subtract_fusion
  1.3 0.6 reshape.12.pos_ref
  1.9 20.1 %front.1 = (bf16[2304,1024]{1,0:T(8,128)(2,1)}, bf16[768,768]{1,0:T(8,128)(2,1)}, f32[384,1024]{1,0:T(8,128)}, f32[8,384]{1,0:T(8,128)}) custom-call(f32[384,768]{1,0:T(8,128)} %q_ref.1, s32[96,1024]{1,0:T(8,128)} %bitcast.2, s32[1,384]{1,0:T(1,128)} %reshape.12.pos_ref, f32[256,768]{1,0:T(8,128)} %book_ref.1), custom_call_target="tpu_custom_call" | custom-call | tf_op jit(solution)/shard_map/front/pallas_call | solution.py:475
  21.9 71.2 %back.1 = (f32[384,768]{1,0:T(8,128)}, f32[768,256]{1,0:T(8,128)}, f32[1,384]{1,0:T(1,128)}) custom-call(bf16[2304,1024]{1,0:T(8,128)(2,1)} %get-tuple-element.10.r3, bf16[768,768]{1,0:T(8,128)(2,1)} %get-tuple-element.11.q_t, s32[96,1024]{1,0:T(8,128)} %bitcast.3, f32[384,1024]{1,0:T(8,128)} %get-tuple-element.12.e_ref, s32[1,384]{1,0:T(1,128)} %reshape.12.pos_ref, ...), custom_call_target="tpu_custom_call" | custom-call | tf_op jit(solution)/shard_map/back/pallas_call | solution.py:494
  93.1 0.0 copy-start.1
  93.1 0.0 copy-start
  93.1 2.4 %copy.7 = f32[256,768]{1,0:T(8,128)} copy(f32[256,768]{0,1:T(8,128)} %bitcast.4) | data formatting | bytes 1572864
  95.5 0.0 copy-done.1
  95.5 0.6 reduce
  96.1 0.0 copy-done
  96.1 1.0 %copy.9 = f32[384,768]{1,0:T(8,128)} copy(f32[384,768]{1,0:T(8,128)S(1)} %copy-done) | data formatting | bytes 2359296
Async XLA Ops:
  93.1 2.4 %copy-start.1 = (f32[1,384]{1,0:T(1,128)S(1)}, f32[1,384]{1,0:T(1,128)}, u32[]{:S(2)}) copy-start(f32[1,384]{1,0:T(1,128)} %get-tuple-element.16) | copy-start | bytes 4612
  93.1 3.0 %copy-start = (f32[384,768]{1,0:T(8,128)S(1)}, f32[384,768]{1,0:T(8,128)}, u32[]{:S(2)}) copy-start(f32[384,768]{1,0:T(8,128)} %get-tuple-element.23) | copy-start | bytes 3538948

commit v2 on v1

v2 whole, which is shorter than its diff:
```python
import jax
import jax.numpy as jnp
from jax import lax
from jax.experimental import pallas as pl
from jax.experimental.pallas import tpu as pltpu
from jax.sharding import PartitionSpec as P

F32, BF16, I32 = jnp.float32, jnp.bfloat16, jnp.int32
NN = (((1,), (0,)), ((), ()))
NT = (((1,), (1,)), ((), ()))
HIGH_CODES = 64
LOW_CODES = 4


def dot(a, b, dims=NN):
    return lax.dot_general(a, b, dims, preferred_element_type=F32)


def split(x):
    high = x.astype(BF16)
    return high, (x - high.astype(F32)).astype(BF16)


def split3(x):
    high = x.astype(BF16)
    rest = x - high.astype(F32)
    mid = rest.astype(BF16)
    return high, mid, (rest - mid.astype(F32)).astype(BF16)


def split_queries(q_ref, q3, step=32):
    width = q_ref.shape[1]

    def block(b, _):
        at = pl.ds(pl.multiple_of(b * step, step), step)
        high, mid, low = split3(q_ref[at, :])
        q3[at, :width] = high
        q3[at, width : 2 * width] = mid
        q3[at, 2 * width :] = low
        return 0

    lax.fori_loop(0, q_ref.shape[0] // step, block, 0)


def transpose_queries(q_ref, q_t, step=128):
    rows = q_ref.shape[0]

    def block(b, _):
        at = pl.ds(pl.multiple_of(b * step, step), step)
        high, mid = split(q_ref[:, at].T)
        q_t[at, :rows] = high
        q_t[at, rows : 2 * rows] = mid
        q_t[at, 2 * rows :] = high
        return 0

    lax.fori_loop(0, q_ref.shape[1] // step, block, 0)


def transpose_book(book_ref, book_t, step=128):
    def block(b, _):
        at = pl.ds(pl.multiple_of(b * step, step), step)
        book_t[at, :] = book_ref[:, at].T
        return 0

    lax.fori_loop(0, book_ref.shape[1] // step, block, 0)


def rebuild(codes_t, book_t, r3, unroll=4):
    subs, docs = codes_t.shape
    width = book_t.shape[0]
    sub_width = width // subs

    def pair(p):
        parts = []
        for side in range(2):
            m = 2 * p + side
            base = pl.multiple_of(m * sub_width, sub_width)
            low = book_t[pl.ds(base, sub_width), :128]
            high = book_t[pl.ds(base, sub_width), 128:]
            code = codes_t[pl.ds(m, 1), :]
            tiles = []
            for t in range(docs // 128):
                picked = jnp.broadcast_to(code[:, 128 * t : 128 * t + 128], (sub_width, 128))
                lane = picked & 127
                a = jnp.take_along_axis(low, lane, axis=1, mode="promise_in_bounds")
                b = jnp.take_along_axis(high, lane, axis=1, mode="promise_in_bounds")
                tiles.append(jnp.where(picked < 128, a, b))
            parts.append(jnp.concatenate(tiles, axis=1))
        high, mid, low = split3(jnp.concatenate(parts, axis=0))
        at = pl.multiple_of(2 * p * sub_width, 2 * sub_width)
        r3[pl.ds(at, 2 * sub_width), :] = low
        r3[pl.ds(width + at, 2 * sub_width), :] = mid
        r3[pl.ds(2 * width + at, 2 * sub_width), :] = high

    def block(b, _):
        for u in range(unroll):
            pair(unroll * b + u)
        return 0

    lax.fori_loop(0, subs // 2 // unroll, block, 0)


def score(q3, r3, s_ref, tile=256):
    width = q3.shape[1] // 3

    def block(t, _):
        at = pl.ds(pl.multiple_of(t * tile, tile), tile)
        acc = dot(q3[...], r3[:, at])
        acc = acc + dot(q3[:, : 2 * width], r3[width:, at])
        acc = acc + dot(q3[:, :width], r3[2 * width :, at])
        s_ref[:, at] = acc
        return 0

    lax.fori_loop(0, s_ref.shape[1] // tile, block, 0)


def statistics(s_ref, pos_col, cols, step=64):
    rows, docs = s_ref.shape
    lane = lax.broadcasted_iota(I32, (step, 128), 1)
    ids = lax.broadcasted_iota(I32, (step, docs), 1)

    def block(b, _):
        at = pl.ds(pl.multiple_of(b * step, step), step)
        s = s_ref[at, :]
        top = jnp.max(s, axis=1, keepdims=True)
        own = jnp.sum(jnp.where(pos_col[at, :1] == ids, s, 0.0), axis=1, keepdims=True)
        e = jnp.exp(s - top)
        total = jnp.sum(e, axis=1, keepdims=True)
        s_ref[at, :] = e
        cols[at, :] = jnp.where(
            lane == 0, top, jnp.where(lane == 1, total, jnp.where(lane == 2, own, 0.0))
        )
        return 0

    lax.fori_loop(0, rows // step, block, 0)


def as_column(row, column):
    column[...] = jnp.broadcast_to(row, (128, row.shape[1])).T


def expose(e_ref, pos_col, e2, hits, step=32):
    rows, docs = e_ref.shape
    ids = lax.broadcasted_iota(I32, (step, docs), 1)

    def block(b, _):
        at = pl.ds(pl.multiple_of(b * step, step), step)
        high, low = split(e_ref[at, :])
        e2[at, :] = low
        e2[pl.ds(pl.multiple_of(rows + b * step, step), step), :] = high
        hits[at, :] = jnp.where(pos_col[at, :1] == ids, 1.0, 0.0).astype(BF16)
        return 0

    lax.fori_loop(0, rows // step, block, 0)


def query_products(e2, hits, r3, spread, pulled, tile=256):
    rows = hits.shape[0]
    width = r3.shape[0] // 3

    def block(t, _):
        base = pl.multiple_of(t * tile, tile)
        mid = r3[pl.ds(width + base, tile), :]
        high = r3[pl.ds(2 * width + base, tile), :]
        acc = dot(e2[rows:, :], mid, NT)
        acc = acc + dot(e2[:rows, :], high, NT)
        spread[:, pl.ds(base, tile)] = acc + dot(e2[rows:, :], high, NT)
        pull = dot(hits[...], r3[pl.ds(base, tile), :], NT)
        pull = pull + dot(hits[...], mid, NT)
        pulled[:, pl.ds(base, tile)] = pull + dot(hits[...], high, NT)
        return 0

    lax.fori_loop(0, width // tile, block, 0)


def query_gradient(spread, pulled, scale_col, out, step=32):
    def block(b, _):
        at = pl.ds(pl.multiple_of(b * step, step), step)
        out[at, :] = spread[at, :] * scale_col[at, :1] - pulled[at, :]
        return 0

    lax.fori_loop(0, spread.shape[0] // step, block, 0)


def weigh(e_ref, scale_col, pos_col, w3, step=32):
    rows, docs = e_ref.shape
    ids = lax.broadcasted_iota(I32, (step, docs), 1)

    def block(b, _):
        at = pl.ds(pl.multiple_of(b * step, step), step)
        w = e_ref[at, :] * scale_col[at, :1]
        w = w - jnp.where(pos_col[at, :1] == ids, 1.0, 0.0)
        high, low = split(w)
        w3[at, :] = low
        w3[pl.ds(pl.multiple_of(rows + b * step, step), step), :] = high
        w3[pl.ds(pl.multiple_of(2 * rows + b * step, step), step), :] = high
        return 0

    lax.fori_loop(0, rows // step, block, 0)


def document_gradient(w3, q_t, out, tile=256):
    def block(t, _):
        at = pl.ds(pl.multiple_of(t * tile, tile), tile)
        out[:, at] = dot(q_t[...], w3[:, at])
        return 0

    lax.fori_loop(0, out.shape[1] // tile, block, 0)


def collect(codes_t, d_ref, out, blocks, base, group=4, unroll=2):
    subs, docs = codes_t.shape
    sub_width = d_ref.shape[0] // subs
    word = lax.broadcasted_iota(I32, (HIGH_CODES, docs), 0)
    lane = lax.broadcasted_iota(I32, (sub_width, 128), 1)

    def one(b):
        g = lax.rem(b + base, subs // group)
        tables, values = [], []
        for s in range(group):
            m = group * g + s
            code = codes_t[pl.ds(m, 1), :]
            inner = code & (HIGH_CODES - 1)
            outer = jnp.broadcast_to(code >> 6, (sub_width, docs))
            tables.append(jnp.where(word == inner, 1.0, 0.0).astype(BF16))
            d = d_ref[pl.ds(pl.multiple_of(m * sub_width, sub_width), sub_width), :]
            high = d.astype(BF16).astype(F32)
            low = d - high
            masks = [outer == k for k in range(LOW_CODES)]
            rows = [jnp.where(mask, part, 0.0) for part in (high, low) for mask in masks]
            values.append(jnp.concatenate(rows, axis=0).astype(BF16))
        found = dot(jnp.concatenate(values, axis=0), jnp.concatenate(tables, axis=0), NT)
        rows = 2 * LOW_CODES * sub_width
        for s in range(group):
            at = 128 * (s // 2)
            piece = found[rows * s : rows * (s + 1), at : at + 128]
            piece = piece[: rows // 2] + piece[rows // 2 :]
            parts = [piece[sub_width * k : sub_width * (k + 1)] for k in range(LOW_CODES)]
            start = pl.multiple_of((group * g + s) * sub_width, sub_width)
            for k in range(2):
                first, second = parts[2 * k], parts[2 * k + 1]
                if s % 2:
                    first = pltpu.roll(first, 64, 1)
                else:
                    second = pltpu.roll(second, 64, 1)
                out[pl.ds(start, sub_width), 128 * k : 128 * k + 128] = jnp.where(
                    lane < 64, first, second
                )

    def block(b, _):
        for u in range(unroll):
            one(unroll * b + u)
        return 0

    lax.fori_loop(blocks[0] // unroll, blocks[1] // unroll, block, 0)


def transpose_half(part, core, out, step=128):
    half = part.shape[0] // 2

    def block(b, _):
        at = pl.ds(pl.multiple_of(core * half + b * step, step), step)
        out[:, at] = part[at, :].T
        return 0

    lax.fori_loop(0, half // step, block, 0)


class Place:
    def __init__(self):
        query, corpus = lax.axis_index("query"), lax.axis_index("corpus")
        self.y = lax.rem(query, 4)
        self.x = 2 * lax.div(query, 4) + lax.rem(lax.div(corpus, 2), 2)
        self.z = lax.div(corpus, 4)
        self.core = lax.rem(corpus, 2)

    def at(self, x=None, y=None, z=None, core=None):
        x = self.x if x is None else x
        y = self.y if y is None else y
        z = self.z if z is None else z
        core = self.core if core is None else core
        return (4 * lax.div(x, 2) + y, 4 * z + 2 * lax.rem(x, 2) + core)

    def next_y(self, d):
        return lax.rem(self.y + d, 4)

    def next_x(self, d):
        return lax.rem(self.x + d, 4)

    def next_z(self, d):
        return lax.rem(self.z + d, 8)


class Wire:
    def __init__(self, sent, arrived):
        self.sent, self.arrived, self.copies = sent, arrived, []

    def send(self, src, dst, device):
        i = len(self.copies)
        copy = pltpu.make_async_remote_copy(
            src_ref=src,
            dst_ref=dst,
            send_sem=self.sent.at[i],
            recv_sem=self.arrived.at[i],
            device_id=device,
            device_id_type=pl.DeviceIdType.MESH,
        )
        copy.start()
        self.copies.append(copy)
        return copy

    def finish(self):
        for copy in self.copies:
            copy.wait_send()


def rows_at(index, size):
    return pl.ds(pl.multiple_of(index * size, size), size)


def merge(stats):
    top = stats[0][0:1]
    for s in stats[1:]:
        top = jnp.maximum(top, s[0:1])
    total = sum(s[1:2] * jnp.exp(s[0:1] - top) for s in stats)
    own = sum(s[2:3] for s in stats)
    pad = jnp.zeros((8 - 3, top.shape[1]), F32)
    return jnp.concatenate([top, total, own, pad], axis=0)


def step(
    q_ref, codes_t, pos_ref, book_ref,
    grad_q, grad_b, loss_ref,
    book_t, q3, r3, q_t, e_ref, stats_ref, cols,
    pos_col, scale_col, e2, hits, spread, pulled, w3, d_ref,
    near, far, part_q, half_q, sum_q, up, down, cross,
    words_b, part_b, half_b, sum_b, first_in, first_sum, second_in, second_sum, last_in,
    sent, arrived,
):
    me = Place()
    wire = Wire(sent, arrived)
    x_pair = me.x + 1 - 2 * lax.rem(me.x, 2)
    other = 1 - me.core
    partners = [me.at(core=other), me.at(x=x_pair), me.at(x=x_pair, core=other)]
    far_partners = [me.at(z=me.next_z(d)) for d in range(1, 8)]
    y_partners = [me.at(y=me.next_y(d)) for d in range(1, 4)]
    x_partners = [me.at(x=me.next_x(d)) for d in range(1, 4)]
    greeted = [partners[0], partners[2]] + far_partners + y_partners + x_partners
    barrier = pltpu.get_barrier_semaphore()
    for device in greeted:
        pl.semaphore_signal(barrier, inc=1, device_id=device, device_id_type=pl.DeviceIdType.MESH)

    transpose_book(book_ref, book_t)
    split_queries(q_ref, q3)
    rebuild(codes_t, book_t, r3)
    score(q3, r3, e_ref)
    docs = codes_t.shape[1]
    here = pos_ref[...] - lax.axis_index("corpus") * docs
    as_column(here, pos_col)
    statistics(e_ref, pos_col, cols)
    stats_ref[...] = cols[...].T[:8]
    pl.semaphore_wait(barrier, len(greeted))

    mine = 2 * lax.rem(me.x, 2) + me.core
    near[mine] = stats_ref[...]
    copies = [wire.send(stats_ref, near.at[mine], device) for device in partners]
    expose(e_ref, pos_col, e2, hits)
    for copy in copies:
        copy.wait_recv()
    far[me.z] = merge([near[k] for k in range(4)])
    copies = [wire.send(far.at[me.z], far.at[me.z], device) for device in far_partners]
    query_products(e2, hits, r3, spread, pulled)
    transpose_queries(q_ref, q_t)
    for copy in copies:
        copy.wait_recv()
    whole = merge([far[k] for k in range(8)])
    log_total = whole[0:1] + jnp.log(whole[1:2])
    loss_ref[...] = log_total - whole[2:3]
    as_column(jnp.exp(stats_ref[0:1] - log_total), scale_col)

    query_gradient(spread, pulled, scale_col, part_q)
    half = part_q.shape[0] // 2
    chunk = half // 8
    q_core = wire.send(part_q.at[rows_at(other, half)], half_q, partners[0])
    weigh(e_ref, scale_col, pos_col, w3)
    document_gradient(w3, q_t, d_ref)
    q_core.wait_recv()
    sum_q[...] = part_q[rows_at(me.core, half)] + half_q[...]

    z_up, z_down = far_partners[0], far_partners[6]

    def ring_send(step):
        copies = []
        for buffers, ahead, steps, device in ((up, 4 - step, 4, z_up), (down, 8 - 3 + step, 3, z_down)):
            if step >= steps:
                continue
            at = rows_at(me.next_z(ahead), chunk)
            if step == 0:
                src = sum_q.at[at]
            else:
                src = buffers.at[step - 1]
                src[...] = src[...] + sum_q[at]
            copies.append(wire.send(src, buffers.at[step], device))
        return copies

    def arrive(copies):
        for copy in copies:
            copy.wait_recv()

    subs = codes_t.shape[0]
    groups = subs // 4
    base = other * (groups // 2)
    words, b_half = part_b.shape[0], part_b.shape[1] // 2

    ring = ring_send(0)
    collect(codes_t, d_ref, words_b, (0, groups // 2), base)
    transpose_half(words_b, other, part_b)
    b_core = wire.send(part_b.at[:, rows_at(other, b_half)], half_b, partners[0])
    arrive(ring)
    ring = ring_send(1)
    collect(codes_t, d_ref, words_b, (groups // 2, groups), base)
    transpose_half(words_b, me.core, part_b)
    arrive(ring)
    ring = ring_send(2)
    b_core.wait_recv()
    sum_b[...] = part_b[:, rows_at(me.core, b_half)] + half_b[...]

    lines = words // 8

    def lines_at(k, first, size, second=None):
        start = k * (words // 2) + first * lines
        if second is not None:
            start = start + second * size
        return pl.ds(pl.multiple_of(start, size), size)

    order = (
        ((me.y, me.next_y, y_partners), (me.x, me.next_x, x_partners)),
        ((me.x, me.next_x, x_partners), (me.y, me.next_y, y_partners)),
    )
    firsts = []
    for k in range(2):
        _, following, devices = order[k][0]
        for d in range(1, 4):
            firsts.append(
                wire.send(
                    sum_b.at[lines_at(k, following(d), lines)],
                    first_in.at[k, d - 1],
                    devices[d - 1],
                )
            )
    arrive(ring)
    ring = ring_send(3)
    arrive(firsts)
    seconds = []
    for k in range(2):
        index, _, _ = order[k][0]
        acc = sum_b[lines_at(k, index, lines)]
        for d in range(3):
            acc = acc + first_in[k, d]
        first_sum[k] = acc
        _, following, devices = order[k][1]
        for d in range(1, 4):
            seconds.append(
                wire.send(
                    first_sum.at[k, rows_at(following(d), lines // 4)],
                    second_in.at[k, d - 1],
                    devices[d - 1],
                )
            )

    arrive(ring)
    cross[0] = sum_q[rows_at(me.z, chunk)] + (up[3] + down[2])
    across = wire.send(cross.at[0], cross.at[1], partners[1])

    arrive(seconds)
    for k in range(2):
        index, _, _ = order[k][1]
        acc = first_sum[k, rows_at(index, lines // 4)]
        for d in range(3):
            acc = acc + second_in[k, d]
        last_in[me.z, k] = acc
    lasts = [wire.send(last_in.at[me.z], last_in.at[me.z], device) for device in far_partners]

    def q_rows(z):
        return pl.ds(pl.multiple_of(me.core * half + z * chunk, chunk), chunk)

    passed = []

    def pass_on(hop):
        copies = []
        for back_by, hops, device in ((8 - hop, 4, z_up), (hop, 3, z_down)):
            if hop < hops:
                at = q_rows(me.next_z(back_by))
                copies.append(wire.send(grad_q.at[at], grad_q.at[at], device))
        return copies

    def to_core(hop):
        for ahead, hops in ((8 - hop - 1, 4), (hop + 1, 3)):
            if hop < hops:
                at = q_rows(me.next_z(ahead))
                passed.append(wire.send(grad_q.at[at], grad_q.at[at], partners[0]))

    arrive([across])
    grad_q[q_rows(me.z)] = cross[0] + cross[1]
    ring = pass_on(0)
    passed.append(wire.send(grad_q.at[q_rows(me.z)], grad_q.at[q_rows(me.z)], partners[0]))

    columns = rows_at(me.core, b_half)
    arrive(lasts)
    acc = last_in[0]
    for z in range(1, 8):
        acc = acc + last_in[z]
    seconds = []
    for k in range(2):
        at = lines_at(k, order[k][0][0], lines // 4, order[k][1][0])
        grad_b[at, columns] = acc[k]
        for device in order[k][1][2]:
            seconds.append(wire.send(grad_b.at[at, columns], grad_b.at[at, columns], device))
    arrive(ring)
    ring = pass_on(1)
    to_core(0)
    arrive(seconds)
    firsts = []
    for k in range(2):
        at = lines_at(k, order[k][0][0], lines)
        for device in order[k][0][2]:
            firsts.append(wire.send(grad_b.at[at, columns], grad_b.at[at, columns], device))
    arrive(ring)
    ring = pass_on(2)
    to_core(1)
    arrive(firsts)
    passed.append(wire.send(grad_b.at[:, columns], grad_b.at[:, columns], partners[0]))
    arrive(ring)
    ring = pass_on(3)
    to_core(2)
    arrive(ring)
    to_core(3)
    arrive(passed)
    wire.finish()


def local(queries, codes, positive, codebook):
    rows, width = queries.shape
    docs, subs = codes.shape
    words = codebook.shape[0]
    chunk = rows // 16
    lines = words // 8
    half = width // 2
    vmem = pl.BlockSpec(memory_space=pltpu.VMEM)
    grad_q, grad_b, loss = pl.pallas_call(
        step,
        in_specs=[vmem] * 4,
        out_specs=(vmem, vmem, vmem),
        out_shape=(
            jax.ShapeDtypeStruct((rows, width), F32),
            jax.ShapeDtypeStruct((words, width), F32),
            jax.ShapeDtypeStruct((1, rows), F32),
        ),
        scratch_shapes=[
            pltpu.VMEM((width, words), F32),
            pltpu.VMEM((rows, 3 * width), BF16),
            pltpu.VMEM((3 * width, docs), BF16),
            pltpu.VMEM((width, 3 * rows), BF16),
            pltpu.VMEM((rows, docs), F32),
            pltpu.VMEM((8, rows), F32),
            pltpu.VMEM((rows, 128), F32),
            pltpu.VMEM((rows, 128), I32),
            pltpu.VMEM((rows, 128), F32),
            pltpu.VMEM((2 * rows, docs), BF16),
            pltpu.VMEM((rows, docs), BF16),
            pltpu.VMEM((rows, width), F32),
            pltpu.VMEM((rows, width), F32),
            pltpu.VMEM((3 * rows, docs), BF16),
            pltpu.VMEM((width, docs), F32),
            pltpu.VMEM((4, 8, rows), F32),
            pltpu.VMEM((8, 8, rows), F32),
            pltpu.VMEM((rows, width), F32),
            pltpu.VMEM((rows // 2, width), F32),
            pltpu.VMEM((rows // 2, width), F32),
            pltpu.VMEM((4, chunk, width), F32),
            pltpu.VMEM((3, chunk, width), F32),
            pltpu.VMEM((2, chunk, width), F32),
            pltpu.VMEM((width, words), F32),
            pltpu.VMEM((words, width), F32),
            pltpu.VMEM((words, half), F32),
            pltpu.VMEM((words, half), F32),
            pltpu.VMEM((2, 3, lines, half), F32),
            pltpu.VMEM((2, lines, half), F32),
            pltpu.VMEM((2, 3, lines // 4, half), F32),
            pltpu.VMEM((2, lines // 4, half), F32),
            pltpu.VMEM((8, 2, lines // 4, half), F32),
            pltpu.SemaphoreType.DMA((80,)),
            pltpu.SemaphoreType.DMA((80,)),
        ],
        compiler_params=pltpu.CompilerParams(collective_id=0, has_side_effects=True),
        name="step",
    )(queries, codes.T, positive.reshape(1, rows), codebook)
    return grad_q, grad_b, loss.reshape(rows)


def solution(mesh):
    return jax.shard_map(
        local,
        mesh=mesh,
        in_specs=(P("query", None), P("corpus", None), P("query"), P()),
        out_specs=(P("query", None), P(), P("query")),
        check_vma=False,
    )
```

time: 97.3 us -> 80.6 us (0.83)
  Pallas kernels: 91.2 us -> 73.9 us
    pallas_call x2 -> x1, Pallas kernels: 91.2 us -> 73.9 us  [local(): pl.pallas_call(step, in_specs=[vmem] * 4, out_specs=(vmem, vmem, vmem), o...]
    unnamed x6 -> x4, local copies, waits for them, and re-layouts: 3.4 us -> 3.32 us
where the time goes in v2:
time: 80.6 us; the launch traced here: 80.4 us
  Pallas kernels  73.9 us (92%)
  local copies, waits for them, and re-layouts  4.56 us (6%)
  other arithmetic  1.27 us (2%)
    pallas_call x1, Pallas kernels, local(): pl.pallas_call(step, in_specs=[vmem] * 4, out_specs=(vmem, vmem, vmem), o...  73.9 us
    unnamed x4, local copies, waits for them, and re-layouts  3.32 us

profile of v2, /device:TPU:1, one launch (start us, length us, event | category | flops | bytes accessed | tf_op | source)
XLA Modules:
  0.0 80.4 jit_solution(1145891001667833939)
XLA Ops:
  0.6 1.2 %reshape.12.pos_ref = s32[1,384]{1,0:T(1,128)} reshape(s32[384]{0:T(512)} %param.6) | data formatting | bytes 3072 | tf_op jit(solution)/shard_map/reshape | solution.py:597
  1.9 73.9 %step.1 = (f32[384,768]{1,0:T(8,128)}, f32[256,768]{1,0:T(8,128)}, f32[1,384]{1,0:T(1,128)}) custom-call(f32[384,768]{1,0:T(8,128)} %q_ref.1, s32[96,1024]{1,0:T(8,128)} %bitcast.1, s32[1,384]{1,0:T(1,128)} %reshape.12.pos_ref, f32[256,768]{1,0:T(8,128)} %book_ref.1), custom_call_target="tpu_custom_call" | custom-call | tf_op jit(solution)/shard_map/step/pallas_call | solution.py:550
  75.8 1.3 %reduce = f32[384]{0:T(512)} reduce(f32[1,384]{1,0:T(1,128)} %get-tuple-element.8, f32[]{:T(128)} %constant), dimensions={0}, to_apply=%get-tuple-element.8.reduce_sub_computation | reduce | bytes 3076 | tf_op jit(solution)/shard_map/step/pallas_call | solution.py:550
  77.1 0.0 copy-start
  77.1 2.4 %copy.9 = f32[384,768]{1,0:T(8,128)} copy(f32[384,768]{1,0:T(8,128)} %get-tuple-element.12) | data formatting | bytes 2359296
  79.5 0.0 copy-done
  79.5 0.9 %copy.10 = f32[256,768]{1,0:T(8,128)} copy(f32[256,768]{1,0:T(8,128)S(1)} %copy-done) | data formatting | bytes 1572864
Async XLA Ops:
  77.1 2.4 %copy-start = (f32[256,768]{1,0:T(8,128)S(1)}, f32[256,768]{1,0:T(8,128)}, u32[]{:S(2)}) copy-start(f32[256,768]{1,0:T(8,128)} %get-tuple-element.13) | copy-start | bytes 2359300

commit v3 on v2

--- a/solution.py
+++ b/solution.py
@@ -10,6 +10,8 @@
 NT = (((1,), (1,)), ((), ()))
 HIGH_CODES = 64
 LOW_CODES = 4
+UNROLL = 6
+COPIES = 102
 
 
 def dot(a, b, dims=NN):
@@ -50,7 +52,8 @@
         high, mid = split(q_ref[:, at].T)
         q_t[at, :rows] = high
         q_t[at, rows : 2 * rows] = mid
-        q_t[at, 2 * rows :] = high
+        q_t[at, 2 * rows : 3 * rows] = high
+        q_t[at, 3 * rows :] = jnp.zeros((step, q_t.shape[1] - 3 * rows), BF16)
         return 0
 
     lax.fori_loop(0, q_ref.shape[1] // step, block, 0)
@@ -100,15 +103,14 @@
     lax.fori_loop(0, subs // 2 // unroll, block, 0)
 
 
-def score(q3, r3, s_ref, tile=256):
+def score(q3, r3, s_ref, tile=512):
     width = q3.shape[1] // 3
 
     def block(t, _):
         at = pl.ds(pl.multiple_of(t * tile, tile), tile)
         acc = dot(q3[...], r3[:, at])
         acc = acc + dot(q3[:, : 2 * width], r3[width:, at])
-        acc = acc + dot(q3[:, :width], r3[2 * width :, at])
-        s_ref[:, at] = acc
+        s_ref[:, at] = acc + dot(q3[:, :width], r3[2 * width :, at])
         return 0
 
     lax.fori_loop(0, s_ref.shape[1] // tile, block, 0)
@@ -154,8 +156,20 @@
     lax.fori_loop(0, rows // step, block, 0)
 
 
-def query_products(e2, hits, r3, spread, pulled, tile=256):
-    rows = hits.shape[0]
+def pull(hits, r3, pulled, tile=256):
+    width = r3.shape[0] // 3
+
+    def block(t, _):
+        base = pl.multiple_of(t * tile, tile)
+        acc = dot(hits[...], r3[pl.ds(width + base, tile), :], NT)
+        pulled[:, pl.ds(base, tile)] = acc + dot(hits[...], r3[pl.ds(2 * width + base, tile), :], NT)
+        return 0
+
+    lax.fori_loop(0, width // tile, block, 0)
+
+
+def spread_out(e2, r3, spread, tile=256):
+    rows = e2.shape[0] // 2
     width = r3.shape[0] // 3
 
     def block(t, _):
@@ -165,9 +179,6 @@
         acc = dot(e2[rows:, :], mid, NT)
         acc = acc + dot(e2[:rows, :], high, NT)
         spread[:, pl.ds(base, tile)] = acc + dot(e2[rows:, :], high, NT)
-        pull = dot(hits[...], r3[pl.ds(base, tile), :], NT)
-        pull = pull + dot(hits[...], mid, NT)
-        pulled[:, pl.ds(base, tile)] = pull + dot(hits[...], high, NT)
         return 0
 
     lax.fori_loop(0, width // tile, block, 0)
@@ -184,6 +195,7 @@
 
 def weigh(e_ref, scale_col, pos_col, w3, step=32):
     rows, docs = e_ref.shape
+    w3[3 * rows :, :] = jnp.zeros((w3.shape[0] - 3 * rows, docs), BF16)
     ids = lax.broadcasted_iota(I32, (step, docs), 1)
 
     def block(b, _):
@@ -200,15 +212,12 @@
 
 
 def document_gradient(w3, q_t, out, tile=256):
-    def block(t, _):
-        at = pl.ds(pl.multiple_of(t * tile, tile), tile)
+    for t in range(out.shape[1] // tile):
+        at = slice(t * tile, t * tile + tile)
         out[:, at] = dot(q_t[...], w3[:, at])
-        return 0
-
-    lax.fori_loop(0, out.shape[1] // tile, block, 0)
-
-
-def collect(codes_t, d_ref, out, blocks, base, group=4, unroll=2):
+
+
+def collect(codes_t, d_ref, out, blocks, base, group=4, unroll=UNROLL):
     subs, docs = codes_t.shape
     sub_width = d_ref.shape[0] // subs
     word = lax.broadcasted_iota(I32, (HIGH_CODES, docs), 0)
@@ -355,7 +364,7 @@
     rebuild(codes_t, book_t, r3)
     score(q3, r3, e_ref)
     docs = codes_t.shape[1]
-    here = pos_ref[...] - lax.axis_index("corpus") * docs
+    here = pos_ref[...].reshape(1, -1) - lax.axis_index("corpus") * docs
     as_column(here, pos_col)
     statistics(e_ref, pos_col, cols)
     stats_ref[...] = cols[...].T[:8]
@@ -365,17 +374,18 @@
     near[mine] = stats_ref[...]
     copies = [wire.send(stats_ref, near.at[mine], device) for device in partners]
     expose(e_ref, pos_col, e2, hits)
+    pull(hits, r3, pulled)
     for copy in copies:
         copy.wait_recv()
     far[me.z] = merge([near[k] for k in range(4)])
     copies = [wire.send(far.at[me.z], far.at[me.z], device) for device in far_partners]
-    query_products(e2, hits, r3, spread, pulled)
+    spread_out(e2, r3, spread)
     transpose_queries(q_ref, q_t)
     for copy in copies:
         copy.wait_recv()
     whole = merge([far[k] for k in range(8)])
     log_total = whole[0:1] + jnp.log(whole[1:2])
-    loss_ref[...] = log_total - whole[2:3]
+    loss_ref[...] = (log_total - whole[2:3]).reshape(-1)
     as_column(jnp.exp(stats_ref[0:1] - log_total), scale_col)
 
     query_gradient(spread, pulled, scale_col, part_q)
@@ -485,27 +495,45 @@
         return pl.ds(pl.multiple_of(me.core * half + z * chunk, chunk), chunk)
 
     passed = []
-
-    def pass_on(hop):
+    slices = 3
+    size = chunk // slices
+
+    def q_slice(z, k):
+        return pl.ds(pl.multiple_of(me.core * half + z * chunk + k * size, size), size)
+
+    def share(at, device):
+        return wire.send(grad_q.at[at], grad_q.at[at], device)
+
+    def pass_on(hop, k):
         copies = []
         for back_by, hops, device in ((8 - hop, 4, z_up), (hop, 3, z_down)):
             if hop < hops:
-                at = q_rows(me.next_z(back_by))
-                copies.append(wire.send(grad_q.at[at], grad_q.at[at], device))
+                copies.append(share(q_slice(me.next_z(back_by), k), device))
         return copies
 
-    def to_core(hop):
+    def to_core(hop, k):
         for ahead, hops in ((8 - hop - 1, 4), (hop + 1, 3)):
             if hop < hops:
-                at = q_rows(me.next_z(ahead))
-                passed.append(wire.send(grad_q.at[at], grad_q.at[at], partners[0]))
+                passed.append(share(q_slice(me.next_z(ahead), k), partners[0]))
+
+    def next_hop(ring, hop):
+        following = []
+        for k in range(slices):
+            arrive(ring[k])
+            following.append(pass_on(hop, k) if hop < 4 else [])
+            to_core(hop - 1, k)
+        return following
 
     arrive([across])
     grad_q[q_rows(me.z)] = cross[0] + cross[1]
-    ring = pass_on(0)
-    passed.append(wire.send(grad_q.at[q_rows(me.z)], grad_q.at[q_rows(me.z)], partners[0]))
+    ring = [pass_on(0, k) for k in range(slices)]
+    passed.append(share(q_rows(me.z), partners[0]))
 
     columns = rows_at(me.core, b_half)
+
+    def share_b(at, device):
+        return wire.send(grad_b.at[at, columns], grad_b.at[at, columns], device)
+
     arrive(lasts)
     acc = last_in[0]
     for z in range(1, 8):
@@ -515,28 +543,27 @@
         at = lines_at(k, order[k][0][0], lines // 4, order[k][1][0])
         grad_b[at, columns] = acc[k]
         for device in order[k][1][2]:
-            seconds.append(wire.send(grad_b.at[at, columns], grad_b.at[at, columns], device))
-    arrive(ring)
-    ring = pass_on(1)
-    to_core(0)
+            seconds.append(share_b(at, device))
+    ring = next_hop(ring, 1)
     arrive(seconds)
     firsts = []
     for k in range(2):
         at = lines_at(k, order[k][0][0], lines)
         for device in order[k][0][2]:
-            firsts.append(wire.send(grad_b.at[at, columns], grad_b.at[at, columns], device))
-    arrive(ring)
-    ring = pass_on(2)
-    to_core(1)
-    arrive(firsts)
-    passed.append(wire.send(grad_b.at[:, columns], grad_b.at[:, columns], partners[0]))
-    arrive(ring)
-    ring = pass_on(3)
-    to_core(2)
-    arrive(ring)
-    to_core(3)
+            firsts.append(share_b(at, device))
+    for k in range(2):
+        passed.append(share_b(lines_at(k, order[k][0][0], lines), partners[0]))
+    ring = next_hop(ring, 2)
+    ring = next_hop(ring, 3)
+    for d in (1, 3, 2):
+        for k in range(2):
+            arrive([firsts[3 * k + d - 1]])
+            back = order[k][0][1](4 - d)
+            passed.append(share_b(lines_at(k, back, lines), partners[0]))
+    next_hop(ring, 4)
     arrive(passed)
     wire.finish()
+    assert len(wire.copies) == COPIES, len(wire.copies)
 
 
 def local(queries, codes, positive, codebook):
@@ -546,6 +573,7 @@
     chunk = rows // 16
     lines = words // 8
     half = width // 2
+    depth = 256 * pl.cdiv(3 * rows, 256)
     vmem = pl.BlockSpec(memory_space=pltpu.VMEM)
     grad_q, grad_b, loss = pl.pallas_call(
         step,
@@ -554,13 +582,13 @@
         out_shape=(
             jax.ShapeDtypeStruct((rows, width), F32),
             jax.ShapeDtypeStruct((words, width), F32),
-            jax.ShapeDtypeStruct((1, rows), F32),
+            jax.ShapeDtypeStruct((rows,), F32),
         ),
         scratch_shapes=[
             pltpu.VMEM((width, words), F32),
             pltpu.VMEM((rows, 3 * width), BF16),
             pltpu.VMEM((3 * width, docs), BF16),
-            pltpu.VMEM((width, 3 * rows), BF16),
+            pltpu.VMEM((width, depth), BF16),
             pltpu.VMEM((rows, docs), F32),
             pltpu.VMEM((8, rows), F32),
             pltpu.VMEM((rows, 128), F32),
@@ -570,7 +598,7 @@
             pltpu.VMEM((rows, docs), BF16),
             pltpu.VMEM((rows, width), F32),
             pltpu.VMEM((rows, width), F32),
-            pltpu.VMEM((3 * rows, docs), BF16),
+            pltpu.VMEM((depth, docs), BF16),
             pltpu.VMEM((width, docs), F32),
             pltpu.VMEM((4, 8, rows), F32),
             pltpu.VMEM((8, 8, rows), F32),
@@ -589,13 +617,15 @@
             pltpu.VMEM((2, 3, lines // 4, half), F32),
             pltpu.VMEM((2, lines // 4, half), F32),
             pltpu.VMEM((8, 2, lines // 4, half), F32),
-            pltpu.SemaphoreType.DMA((80,)),
-            pltpu.SemaphoreType.DMA((80,)),
+            pltpu.SemaphoreType.DMA((COPIES,)),
+            pltpu.SemaphoreType.DMA((COPIES,)),
         ],
-        compiler_params=pltpu.CompilerParams(collective_id=0, has_side_effects=True),
+        compiler_params=pltpu.CompilerParams(
+            collective_id=0, has_side_effects=True, vmem_limit_bytes=42 << 20
+        ),
         name="step",
-    )(queries, codes.T, positive.reshape(1, rows), codebook)
-    return grad_q, grad_b, loss.reshape(rows)
+    )(queries, codes.T, positive, codebook)
+    return grad_q, grad_b, loss
 
 
 def solution(mesh):

time: 80.6 us -> 76.9 us (0.954)
  Pallas kernels: 73.9 us -> 69.5 us
  local copies, waits for them, and re-layouts: 4.56 us -> 6.55 us
  other arithmetic: 1.27 us -> 0 us
    pallas_call x1, Pallas kernels: 73.9 us -> 69.5 us  [local(): pl.pallas_call(step, in_specs=[vmem] * 4, out_specs=(vmem, vmem, vmem), o...]
    unnamed x4 -> x11, local copies, waits for them, and re-layouts: 3.32 us -> 6.55 us
    pallas_call x1 -> x0, other arithmetic: 1.27 us -> none  [local(): pl.pallas_call(step, in_specs=[vmem] * 4, out_specs=(vmem, vmem, vmem), o...]
    reshape x1 -> x0, local copies, waits for them, and re-layouts: 1.25 us -> none  [local(): positive.reshape(1, rows)]
where the time goes in v3:
time: 76.9 us; the launch traced here: 76.7 us
  Pallas kernels  69.5 us (90%)
  local copies, waits for them, and re-layouts  6.55 us (9%)
    pallas_call x1, Pallas kernels, local(): pl.pallas_call(step, in_specs=[vmem] * 4, out_specs=(vmem, vmem, vmem), o...  69.5 us
    unnamed x11, local copies, waits for them, and re-layouts  6.55 us

profile of v3, /device:TPU:1, one launch (start us, length us, event | category | flops | bytes accessed | tf_op | source)
XLA Modules:
  0.0 76.7 jit_solution(12793193852068822347)
XLA Ops:
  0.6 0.0 copy-start
  0.6 1.3 %copy-done = f32[384,768]{1,0:T(8,128)S(1)} copy-done((f32[384,768]{1,0:T(8,128)S(1)}, f32[384,768]{1,0:T(8,128)}, u32[]{:S(2)}) %copy-start) | copy-done | bytes 1179672
  1.9 0.0 copy-start.1
  1.9 1.1 %copy-done.1 = f32[256,768]{1,0:T(8,128)S(1)} copy-done((f32[256,768]{1,0:T(8,128)S(1)}, f32[256,768]{1,0:T(8,128)}, u32[]{:S(2)}) %copy-start.1) | copy-done | bytes 786456
  3.0 0.0 copy-start.2
  3.0 1.0 %copy-done.2 = s32[1024,96]{0,1:T(8,128)S(1)} copy-done((s32[1024,96]{0,1:T(8,128)S(1)}, s32[1024,96]{0,1:T(8,128)}, u32[]{:S(2)}) %copy-start.2) | copy-done | bytes 393240
  4.0 0.0 copy-start.3
  4.0 0.7 copy-done.3
  4.7 69.5 %step.1 = (f32[384,768]{1,0:T(8,128)S(1)}, f32[256,768]{1,0:T(8,128)S(1)}, f32[384]{0:T(512)S(1)}) custom-call(f32[384,768]{1,0:T(8,128)S(1)} %copy-done, s32[96,1024]{1,0:T(8,128)S(1)} %bitcast.1, s32[384]{0:T(512)S(1)} %copy-done.3, f32[256,768]{1,0:T(8,128)S(1)} %copy-done.1), custom_call_target="tpu_custom_call" | custom-call | tf_op jit(solution)/shard_map/step/pallas_call | solution.py:578
  74.2 1.0 %copy.10 = f32[384,768]{1,0:T(8,128)} copy(f32[384,768]{1,0:T(8,128)S(1)} %get-tuple-element.6) | data formatting | bytes 2359296
  75.2 0.9 %copy.11 = f32[256,768]{1,0:T(8,128)} copy(f32[256,768]{1,0:T(8,128)S(1)} %get-tuple-element.7) | data formatting | bytes 1572864
  76.1 0.6 copy.12
Async XLA Ops:
  0.6 1.3 %copy-start = (f32[384,768]{1,0:T(8,128)S(1)}, f32[384,768]{1,0:T(8,128)}, u32[]{:S(2)}) copy-start(f32[384,768]{1,0:T(8,128)} %q_ref.1) | copy-start | bytes 3538948
  1.9 1.1 %copy-start.1 = (f32[256,768]{1,0:T(8,128)S(1)}, f32[256,768]{1,0:T(8,128)}, u32[]{:S(2)}) copy-start(f32[256,768]{1,0:T(8,128)} %book_ref.1) | copy-start | bytes 2359300
  3.0 1.0 %copy-start.2 = (s32[1024,96]{0,1:T(8,128)S(1)}, s32[1024,96]{0,1:T(8,128)}, u32[]{:S(2)}) copy-start(s32[1024,96]{0,1:T(8,128)} %param.5) | copy-start | bytes 1179652
  4.0 0.7 copy-start.3

commit v4 on v3

--- a/solution.py
+++ b/solution.py
@@ -338,14 +338,21 @@
 
 
 def step(
-    q_ref, codes_t, pos_ref, book_ref,
+    q_hbm, codes_hbm, pos_ref, book_hbm,
     grad_q, grad_b, loss_ref,
-    book_t, q3, r3, q_t, e_ref, stats_ref, cols,
+    q_ref, codes_t, book_ref, book_t, q3, r3, q_t, e_ref, stats_ref, cols,
     pos_col, scale_col, e2, hits, spread, pulled, w3, d_ref,
     near, far, part_q, half_q, sum_q, up, down, cross,
     words_b, part_b, half_b, sum_b, first_in, first_sum, second_in, second_sum, last_in,
-    sent, arrived,
+    sent, arrived, loaded,
 ):
+    loads = [
+        pltpu.make_async_copy(book_hbm, book_ref, loaded.at[0]),
+        pltpu.make_async_copy(codes_hbm, codes_t, loaded.at[1]),
+        pltpu.make_async_copy(q_hbm, q_ref, loaded.at[2]),
+    ]
+    for load in loads:
+        load.start()
     me = Place()
     wire = Wire(sent, arrived)
     x_pair = me.x + 1 - 2 * lax.rem(me.x, 2)
@@ -359,9 +366,12 @@
     for device in greeted:
         pl.semaphore_signal(barrier, inc=1, device_id=device, device_id_type=pl.DeviceIdType.MESH)
 
+    loads[0].wait()
     transpose_book(book_ref, book_t)
+    loads[1].wait()
+    rebuild(codes_t, book_t, r3)
+    loads[2].wait()
     split_queries(q_ref, q3)
-    rebuild(codes_t, book_t, r3)
     score(q3, r3, e_ref)
     docs = codes_t.shape[1]
     here = pos_ref[...].reshape(1, -1) - lax.axis_index("corpus") * docs
@@ -534,6 +544,7 @@
     def share_b(at, device):
         return wire.send(grad_b.at[at, columns], grad_b.at[at, columns], device)
 
+    ring = next_hop(ring, 1)
     arrive(lasts)
     acc = last_in[0]
     for z in range(1, 8):
@@ -544,7 +555,7 @@
         grad_b[at, columns] = acc[k]
         for device in order[k][1][2]:
             seconds.append(share_b(at, device))
-    ring = next_hop(ring, 1)
+    ring = next_hop(ring, 2)
     arrive(seconds)
     firsts = []
     for k in range(2):
@@ -553,7 +564,6 @@
             firsts.append(share_b(at, device))
     for k in range(2):
         passed.append(share_b(lines_at(k, order[k][0][0], lines), partners[0]))
-    ring = next_hop(ring, 2)
     ring = next_hop(ring, 3)
     for d in (1, 3, 2):
         for k in range(2):
@@ -566,6 +576,14 @@
     assert len(wire.copies) == COPIES, len(wire.copies)
 
 
+def hand_over(*refs):
+    copies = [pltpu.make_async_copy(refs[k], refs[3 + k], refs[6].at[k]) for k in range(3)]
+    for copy in copies:
+        copy.start()
+    for copy in copies:
+        copy.wait()
+
+
 def local(queries, codes, positive, codebook):
     rows, width = queries.shape
     docs, subs = codes.shape
@@ -575,9 +593,10 @@
     half = width // 2
     depth = 256 * pl.cdiv(3 * rows, 256)
     vmem = pl.BlockSpec(memory_space=pltpu.VMEM)
+    hbm = pl.BlockSpec(memory_space=pltpu.HBM)
     grad_q, grad_b, loss = pl.pallas_call(
         step,
-        in_specs=[vmem] * 4,
+        in_specs=[hbm, hbm, vmem, hbm],
         out_specs=(vmem, vmem, vmem),
         out_shape=(
             jax.ShapeDtypeStruct((rows, width), F32),
@@ -585,6 +604,9 @@
             jax.ShapeDtypeStruct((rows,), F32),
         ),
         scratch_shapes=[
+            pltpu.VMEM((rows, width), F32),
+            pltpu.VMEM((subs, docs), I32),
+            pltpu.VMEM((words, width), F32),
             pltpu.VMEM((width, words), F32),
             pltpu.VMEM((rows, 3 * width), BF16),
             pltpu.VMEM((3 * width, docs), BF16),
@@ -619,13 +641,21 @@
             pltpu.VMEM((8, 2, lines // 4, half), F32),
             pltpu.SemaphoreType.DMA((COPIES,)),
             pltpu.SemaphoreType.DMA((COPIES,)),
+            pltpu.SemaphoreType.DMA((3,)),
         ],
         compiler_params=pltpu.CompilerParams(
-            collective_id=0, has_side_effects=True, vmem_limit_bytes=42 << 20
+            collective_id=0, has_side_effects=True, vmem_limit_bytes=56 << 20
         ),
         name="step",
     )(queries, codes.T, positive, codebook)
-    return grad_q, grad_b, loss
+    return pl.pallas_call(
+        hand_over,
+        in_specs=[vmem] * 3,
+        out_specs=[hbm] * 3,
+        out_shape=[jax.ShapeDtypeStruct(x.shape, F32) for x in (grad_q, grad_b, loss)],
+        scratch_shapes=[pltpu.SemaphoreType.DMA((3,))],
+        name="hand_over",
+    )(grad_q, grad_b, loss)
 
 
 def solution(mesh):

time: 76.9 us -> 76.1 us (0.990)
  local copies, waits for them, and re-layouts: 6.55 us -> 0 us
  Pallas kernels: 69.5 us -> 75.3 us
    unnamed x11 -> x0, local copies, waits for them, and re-layouts: 6.55 us -> none
    pallas_call x1 -> x2, Pallas kernels: 69.5 us -> 75.3 us  [the longest x1 72.4 us: local(): pl.pallas_call(step, in_specs=[hbm, hbm, vmem, hbm], out_specs=(vmem, vme...]
where the time goes in v4:
time: 76.1 us; the launch traced here: 75.9 us
  Pallas kernels  75.3 us (99%)
    pallas_call x1, Pallas kernels, local(): pl.pallas_call(step, in_specs=[hbm, hbm, vmem, hbm], out_specs=(vmem, vme...  72.4 us
    pallas_call x1, Pallas kernels, local(): pl.pallas_call(hand_over, in_specs=[vmem] * 3, out_specs=[hbm] * 3, out_s...  2.81 us

profile of v4, /device:TPU:1, one launch (start us, length us, event | category | flops | bytes accessed | tf_op | source)
XLA Modules:
  0.0 75.9 jit_solution(8599337791783953699)
XLA Ops:
  0.6 72.4 %step.1 = (f32[384,768]{1,0:T(8,128)}, f32[256,768]{1,0:T(8,128)}, f32[384]{0:T(512)}) custom-call(f32[384,768]{1,0:T(8,128)} %q_hbm.1, s32[96,1024]{1,0:T(8,128)} %bitcast.1, s32[384]{0:T(512)} %pos_ref.1, f32[256,768]{1,0:T(8,128)} %book_hbm.1), custom_call_target="tpu_custom_call" | custom-call | tf_op jit(solution)/shard_map/step/pallas_call | solution.py:597
  73.1 2.8 %hand_over.1 = (f32[384,768]{1,0:T(8,128)}, f32[256,768]{1,0:T(8,128)}, f32[384]{0:T(512)}) custom-call(f32[384,768]{1,0:T(8,128)} %get-tuple-element.6.refs_0_, f32[256,768]{1,0:T(8,128)} %get-tuple-element.7.refs_1_, f32[384]{0:T(512)} %get-tuple-element.8.refs_2_), custom_call_target="tpu_custom_call" | custom-call | tf_op jit(solution)/shard_map/hand_over/pallas_call | solution.py:651

commit v5 on v4

--- a/solution.py
+++ b/solution.py
@@ -10,8 +10,7 @@
 NT = (((1,), (1,)), ((), ()))
 HIGH_CODES = 64
 LOW_CODES = 4
-UNROLL = 6
-COPIES = 102
+COPIES = 142
 
 
 def dot(a, b, dims=NN):
@@ -116,7 +115,7 @@
     lax.fori_loop(0, s_ref.shape[1] // tile, block, 0)
 
 
-def statistics(s_ref, pos_col, cols, step=64):
+def statistics(s_ref, pos_col, cols, e2, hits, step=64):
     rows, docs = s_ref.shape
     lane = lax.broadcasted_iota(I32, (step, 128), 1)
     ids = lax.broadcasted_iota(I32, (step, docs), 1)
@@ -125,10 +124,15 @@
         at = pl.ds(pl.multiple_of(b * step, step), step)
         s = s_ref[at, :]
         top = jnp.max(s, axis=1, keepdims=True)
-        own = jnp.sum(jnp.where(pos_col[at, :1] == ids, s, 0.0), axis=1, keepdims=True)
+        hit = pos_col[at, :1] == ids
+        own = jnp.sum(jnp.where(hit, s, 0.0), axis=1, keepdims=True)
+        hits[at, :] = jnp.where(hit, 1.0, 0.0).astype(BF16)
         e = jnp.exp(s - top)
         total = jnp.sum(e, axis=1, keepdims=True)
         s_ref[at, :] = e
+        high, low = split(e)
+        e2[at, :] = low
+        e2[pl.ds(pl.multiple_of(rows + b * step, step), step), :] = high
         cols[at, :] = jnp.where(
             lane == 0, top, jnp.where(lane == 1, total, jnp.where(lane == 2, own, 0.0))
         )
@@ -139,21 +143,6 @@
 
 def as_column(row, column):
     column[...] = jnp.broadcast_to(row, (128, row.shape[1])).T
-
-
-def expose(e_ref, pos_col, e2, hits, step=32):
-    rows, docs = e_ref.shape
-    ids = lax.broadcasted_iota(I32, (step, docs), 1)
-
-    def block(b, _):
-        at = pl.ds(pl.multiple_of(b * step, step), step)
-        high, low = split(e_ref[at, :])
-        e2[at, :] = low
-        e2[pl.ds(pl.multiple_of(rows + b * step, step), step), :] = high
-        hits[at, :] = jnp.where(pos_col[at, :1] == ids, 1.0, 0.0).astype(BF16)
-        return 0
-
-    lax.fori_loop(0, rows // step, block, 0)
 
 
 def pull(hits, r3, pulled, tile=256):
@@ -217,14 +206,14 @@
         out[:, at] = dot(q_t[...], w3[:, at])
 
 
-def collect(codes_t, d_ref, out, blocks, base, group=4, unroll=UNROLL):
+def collect(codes_t, d_ref, out, base, count, group=4):
     subs, docs = codes_t.shape
     sub_width = d_ref.shape[0] // subs
     word = lax.broadcasted_iota(I32, (HIGH_CODES, docs), 0)
     lane = lax.broadcasted_iota(I32, (sub_width, 128), 1)
 
     def one(b):
-        g = lax.rem(b + base, subs // group)
+        g = b + base
         tables, values = [], []
         for s in range(group):
             m = group * g + s
@@ -256,23 +245,17 @@
                     lane < 64, first, second
                 )
 
+    for b in range(count):
+        one(b)
+
+
+def transpose_run(part, base, count, out, step=128):
     def block(b, _):
-        for u in range(unroll):
-            one(unroll * b + u)
-        return 0
-
-    lax.fori_loop(blocks[0] // unroll, blocks[1] // unroll, block, 0)
-
-
-def transpose_half(part, core, out, step=128):
-    half = part.shape[0] // 2
-
-    def block(b, _):
-        at = pl.ds(pl.multiple_of(core * half + b * step, step), step)
+        at = pl.ds(pl.multiple_of(base + b * step, step), step)
         out[:, at] = part[at, :].T
         return 0
 
-    lax.fori_loop(0, half // step, block, 0)
+    lax.fori_loop(0, count // step, block, 0)
 
 
 class Place:
@@ -303,6 +286,7 @@
 class Wire:
     def __init__(self, sent, arrived):
         self.sent, self.arrived, self.copies = sent, arrived, []
+        self.settled, self.mark = 0, 0
 
     def send(self, src, dst, device):
         i = len(self.copies)
@@ -318,8 +302,13 @@
         self.copies.append(copy)
         return copy
 
+    def settle(self):
+        for copy in self.copies[self.settled : self.mark]:
+            copy.wait_send()
+        self.settled, self.mark = self.mark, len(self.copies)
+
     def finish(self):
-        for copy in self.copies:
+        for copy in self.copies[self.settled :]:
             copy.wait_send()
 
 
@@ -376,14 +365,13 @@
     docs = codes_t.shape[1]
     here = pos_ref[...].reshape(1, -1) - lax.axis_index("corpus") * docs
     as_column(here, pos_col)
-    statistics(e_ref, pos_col, cols)
+    statistics(e_ref, pos_col, cols, e2, hits)
     stats_ref[...] = cols[...].T[:8]
     pl.semaphore_wait(barrier, len(greeted))
 
     mine = 2 * lax.rem(me.x, 2) + me.core
     near[mine] = stats_ref[...]
     copies = [wire.send(stats_ref, near.at[mine], device) for device in partners]
-    expose(e_ref, pos_col, e2, hits)
     pull(hits, r3, pulled)
     for copy in copies:
         copy.wait_recv()
@@ -427,25 +415,9 @@
         for copy in copies:
             copy.wait_recv()
 
-    subs = codes_t.shape[0]
-    groups = subs // 4
-    base = other * (groups // 2)
     words, b_half = part_b.shape[0], part_b.shape[1] // 2
-
-    ring = ring_send(0)
-    collect(codes_t, d_ref, words_b, (0, groups // 2), base)
-    transpose_half(words_b, other, part_b)
-    b_core = wire.send(part_b.at[:, rows_at(other, b_half)], half_b, partners[0])
-    arrive(ring)
-    ring = ring_send(1)
-    collect(codes_t, d_ref, words_b, (groups // 2, groups), base)
-    transpose_half(words_b, me.core, part_b)
-    arrive(ring)
-    ring = ring_send(2)
-    b_core.wait_recv()
-    sum_b[...] = part_b[:, rows_at(me.core, b_half)] + half_b[...]
-
     lines = words // 8
+    group_width = 4 * d_ref.shape[0] // codes_t.shape[0]
 
     def lines_at(k, first, size, second=None):
         start = k * (words // 2) + first * lines
@@ -457,54 +429,101 @@
         ((me.y, me.next_y, y_partners), (me.x, me.next_x, x_partners)),
         ((me.x, me.next_x, x_partners), (me.y, me.next_y, y_partners)),
     )
-    firsts = []
-    for k in range(2):
-        _, following, devices = order[k][0]
-        for d in range(1, 4):
-            firsts.append(
-                wire.send(
-                    sum_b.at[lines_at(k, following(d), lines)],
-                    first_in.at[k, d - 1],
-                    devices[d - 1],
+    passed, taken = [], [0, 0]
+
+    def greet_passed():
+        arrive(passed[taken[0] : taken[1]])
+        taken[:] = taken[1], len(passed)
+
+    def gather_words(core, part):
+        offset, count = part
+        base = core * b_half + offset
+        collect(codes_t, d_ref, words_b, core * (b_half // group_width) + offset // group_width, count // group_width)
+        transpose_run(words_b, base, count, part_b)
+
+    def book_chain(part):
+        offset, count = part
+        inner = slice(offset, offset + count)
+        theirs = pl.ds(pl.multiple_of(other * b_half + offset, 128), count)
+        ours = pl.ds(pl.multiple_of(me.core * b_half + offset, 128), count)
+        core = wire.send(part_b.at[:, theirs], half_b.at[:, inner], partners[0])
+        yield
+        core.wait_recv()
+        sum_b[:, inner] = part_b[:, ours] + half_b[:, inner]
+        firsts = []
+        for k in range(2):
+            _, following, devices = order[k][0]
+            for d in range(1, 4):
+                firsts.append(
+                    wire.send(
+                        sum_b.at[lines_at(k, following(d), lines), inner],
+                        first_in.at[k, d - 1, :, inner],
+                        devices[d - 1],
+                    )
                 )
-            )
-    arrive(ring)
-    ring = ring_send(3)
-    arrive(firsts)
-    seconds = []
-    for k in range(2):
-        index, _, _ = order[k][0]
-        acc = sum_b[lines_at(k, index, lines)]
-        for d in range(3):
-            acc = acc + first_in[k, d]
-        first_sum[k] = acc
-        _, following, devices = order[k][1]
-        for d in range(1, 4):
-            seconds.append(
-                wire.send(
-                    first_sum.at[k, rows_at(following(d), lines // 4)],
-                    second_in.at[k, d - 1],
-                    devices[d - 1],
+        yield
+        arrive(firsts)
+        seconds = []
+        for k in range(2):
+            index, _, _ = order[k][0]
+            acc = sum_b[lines_at(k, index, lines), inner]
+            for d in range(3):
+                acc = acc + first_in[k, d, :, inner]
+            first_sum[k, :, inner] = acc
+            _, following, devices = order[k][1]
+            for d in range(1, 4):
+                seconds.append(
+                    wire.send(
+                        first_sum.at[k, rows_at(following(d), lines // 4), inner],
+                        second_in.at[k, d - 1, :, inner],
+                        devices[d - 1],
+                    )
                 )
-            )
-
-    arrive(ring)
-    cross[0] = sum_q[rows_at(me.z, chunk)] + (up[3] + down[2])
-    across = wire.send(cross.at[0], cross.at[1], partners[1])
-
-    arrive(seconds)
-    for k in range(2):
-        index, _, _ = order[k][1]
-        acc = first_sum[k, rows_at(index, lines // 4)]
-        for d in range(3):
-            acc = acc + second_in[k, d]
-        last_in[me.z, k] = acc
-    lasts = [wire.send(last_in.at[me.z], last_in.at[me.z], device) for device in far_partners]
+        yield
+        arrive(seconds)
+        for k in range(2):
+            index, _, _ = order[k][1]
+            acc = first_sum[k, rows_at(index, lines // 4), inner]
+            for d in range(3):
+                acc = acc + second_in[k, d, :, inner]
+            last_in[me.z, k, :, inner] = acc
+        mine = last_in.at[me.z, :, :, inner]
+        lasts = [wire.send(mine, mine, device) for device in far_partners]
+        yield
+        arrive(lasts)
+        acc = last_in[0, :, :, inner]
+        for z in range(1, 8):
+            acc = acc + last_in[z, :, :, inner]
+
+        def share_b(at, device):
+            return wire.send(grad_b.at[at, ours], grad_b.at[at, ours], device)
+
+        seconds = []
+        for k in range(2):
+            at = lines_at(k, order[k][0][0], lines // 4, order[k][1][0])
+            grad_b[at, ours] = acc[k]
+            for device in order[k][1][2]:
+                seconds.append(share_b(at, device))
+        yield
+        arrive(seconds)
+        firsts = []
+        for k in range(2):
+            at = lines_at(k, order[k][0][0], lines)
+            for device in order[k][0][2]:
+                firsts.append(share_b(at, device))
+        for k in range(2):
+            passed.append(share_b(lines_at(k, order[k][0][0], lines), partners[0]))
+        yield
+        for d in (1, 3, 2):
+            for k in range(2):
+                arrive([firsts[3 * k + d - 1]])
+                back = order[k][0][1](4 - d)
+                passed.append(share_b(lines_at(k, back, lines), partners[0]))
+        yield
 
     def q_rows(z):
         return pl.ds(pl.multiple_of(me.core * half + z * chunk, chunk), chunk)
 
-    passed = []
     slices = 3
     size = chunk // slices
 
@@ -521,67 +540,102 @@
                 copies.append(share(q_slice(me.next_z(back_by), k), device))
         return copies
 
-    def to_core(hop, k):
-        for ahead, hops in ((8 - hop - 1, 4), (hop + 1, 3)):
-            if hop < hops:
-                passed.append(share(q_slice(me.next_z(ahead), k), partners[0]))
-
-    def next_hop(ring, hop):
-        following = []
-        for k in range(slices):
-            arrive(ring[k])
-            following.append(pass_on(hop, k) if hop < 4 else [])
-            to_core(hop - 1, k)
-        return following
-
-    arrive([across])
-    grad_q[q_rows(me.z)] = cross[0] + cross[1]
-    ring = [pass_on(0, k) for k in range(slices)]
-    passed.append(share(q_rows(me.z), partners[0]))
-
-    columns = rows_at(me.core, b_half)
-
-    def share_b(at, device):
-        return wire.send(grad_b.at[at, columns], grad_b.at[at, columns], device)
-
-    ring = next_hop(ring, 1)
-    arrive(lasts)
-    acc = last_in[0]
-    for z in range(1, 8):
-        acc = acc + last_in[z]
-    seconds = []
-    for k in range(2):
-        at = lines_at(k, order[k][0][0], lines // 4, order[k][1][0])
-        grad_b[at, columns] = acc[k]
-        for device in order[k][1][2]:
-            seconds.append(share_b(at, device))
-    ring = next_hop(ring, 2)
-    arrive(seconds)
-    firsts = []
-    for k in range(2):
-        at = lines_at(k, order[k][0][0], lines)
-        for device in order[k][0][2]:
-            firsts.append(share_b(at, device))
-    for k in range(2):
-        passed.append(share_b(lines_at(k, order[k][0][0], lines), partners[0]))
-    ring = next_hop(ring, 3)
-    for d in (1, 3, 2):
-        for k in range(2):
-            arrive([firsts[3 * k + d - 1]])
-            back = order[k][0][1](4 - d)
-            passed.append(share_b(lines_at(k, back, lines), partners[0]))
-    next_hop(ring, 4)
-    arrive(passed)
+    def query_chain():
+        ring = ring_send(0)
+        for step in range(1, 4):
+            yield
+            arrive(ring)
+            ring = ring_send(step)
+        yield
+        arrive(ring)
+        cross[0] = sum_q[rows_at(me.z, chunk)] + (up[3] + down[2])
+        across = wire.send(cross.at[0], cross.at[1], partners[1])
+        yield
+        arrive([across])
+        grad_q[q_rows(me.z)] = cross[0] + cross[1]
+        ring = [pass_on(0, k) for k in range(slices)]
+        passed.append(share(q_rows(me.z), partners[0]))
+        for hop in range(1, 5):
+            yield
+            following = []
+            for k in range(slices):
+                arrive(ring[k])
+                following.append(pass_on(hop, k) if hop < 4 else [])
+                for ahead, hops in ((8 - hop, 4), (hop, 3)):
+                    if hop - 1 < hops:
+                        passed.append(share(q_slice(me.next_z(ahead), k), partners[0]))
+            ring = following
+        yield
+
+    large, small = (0, 2 * b_half // 3), (2 * b_half // 3, b_half // 3)
+    queries = query_chain()
+    next(queries)
+    gather_words(other, large)
+    first = book_chain(large)
+    next(first)
+    next(queries)
+    gather_words(me.core, large)
+    next(first)
+    next(queries)
+    gather_words(other, small)
+    second = book_chain(small)
+    next(second)
+    gather_words(me.core, small)
+    next(second)
+    next(queries)
+    wire.settle()
+    next(first)
+    next(second)
+    wire.settle()
+    next(first)
+    next(queries)
+    next(second)
+    next(queries)
+    wire.settle()
+    next(first)
+    next(queries)
+    wire.settle()
+    greet_passed()
+    next(second)
+    next(first)
+    next(queries)
+    wire.settle()
+    greet_passed()
+    next(second)
+    next(first)
+    next(queries)
+    wire.settle()
+    greet_passed()
+    next(second)
+    next(queries)
+    arrive(passed[taken[0] :])
     wire.finish()
     assert len(wire.copies) == COPIES, len(wire.copies)
 
 
 def hand_over(*refs):
-    copies = [pltpu.make_async_copy(refs[k], refs[3 + k], refs[6].at[k]) for k in range(3)]
-    for copy in copies:
-        copy.start()
-    for copy in copies:
-        copy.wait()
+    inside, outside = refs[9], refs[10]
+    steps = []
+    for k in range(3):
+        src, dst, held = refs[k], refs[3 + k], refs[6 + k]
+        pieces = 4 if len(src.shape) > 1 else 1
+        size = src.shape[0] // pieces
+        for n in range(pieces):
+            at = pl.ds(n * size, size)
+            i = len(steps)
+            steps.append(
+                (
+                    pltpu.make_async_copy(src.at[at], held.at[at], inside.at[i]),
+                    pltpu.make_async_copy(held.at[at], dst.at[at], outside.at[i]),
+                )
+            )
+    for load, _ in steps:
+        load.start()
+    for load, store in steps:
+        load.wait()
+        store.start()
+    for _, store in steps:
+        store.wait()
 
 
 def local(queries, codes, positive, codebook):
@@ -650,10 +704,14 @@
     )(queries, codes.T, positive, codebook)
     return pl.pallas_call(
         hand_over,
-        in_specs=[vmem] * 3,
+        in_specs=[hbm] * 3,
         out_specs=[hbm] * 3,
         out_shape=[jax.ShapeDtypeStruct(x.shape, F32) for x in (grad_q, grad_b, loss)],
-        scratch_shapes=[pltpu.SemaphoreType.DMA((3,))],
+        scratch_shapes=[
+            *(pltpu.VMEM(x.shape, F32) for x in (grad_q, grad_b, loss)),
+            pltpu.SemaphoreType.DMA((9,)),
+            pltpu.SemaphoreType.DMA((9,)),
+        ],
         name="hand_over",
     )(grad_q, grad_b, loss)
 

time: 76.1 us -> 76.4 us (level)
  no operation moved by 1% of the time
where the time goes in v5:
time: 76.4 us; the launch traced here: 76.2 us
  Pallas kernels  75.6 us (99%)
    pallas_call x1, Pallas kernels, local(): pl.pallas_call(step, in_specs=[hbm, hbm, vmem, hbm], out_specs=(vmem, vme...  73.2 us
    pallas_call x1, Pallas kernels, local(): pl.pallas_call(hand_over, in_specs=[hbm] * 3, out_specs=[hbm] * 3, out_sh...  2.38 us

profile of v5, /device:TPU:1, one launch (start us, length us, event | category | flops | bytes accessed | tf_op | source)
XLA Modules:
  0.0 76.2 jit_solution(4219898940870384452)
XLA Ops:
  0.6 73.2 %step.1 = (f32[384,768]{1,0:T(8,128)}, f32[256,768]{1,0:T(8,128)}, f32[384]{0:T(512)}) custom-call(f32[384,768]{1,0:T(8,128)} %q_hbm.1, s32[96,1024]{1,0:T(8,128)} %bitcast.1, s32[384]{0:T(512)} %pos_ref.1, f32[256,768]{1,0:T(8,128)} %book_hbm.1), custom_call_target="tpu_custom_call" | custom-call | tf_op jit(solution)/shard_map/step/pallas_call | solution.py:651
  73.8 2.4 %hand_over.1 = (f32[384,768]{1,0:T(8,128)}, f32[256,768]{1,0:T(8,128)}, f32[384]{0:T(512)}) custom-call(f32[384,768]{1,0:T(8,128)} %get-tuple-element.6.refs_0_, f32[256,768]{1,0:T(8,128)} %get-tuple-element.7.refs_1_, f32[384]{0:T(512)} %get-tuple-element.8.refs_2_), custom_call_target="tpu_custom_call" | custom-call | tf_op jit(solution)/shard_map/hand_over/pallas_call | solution.py:705

commit v6 on v5

--- a/solution.py
+++ b/solution.py
@@ -10,7 +10,7 @@
 NT = (((1,), (1,)), ((), ()))
 HIGH_CODES = 64
 LOW_CODES = 4
-COPIES = 142
+COPIES = 114
 
 
 def dot(a, b, dims=NN):
@@ -331,7 +331,7 @@
     grad_q, grad_b, loss_ref,
     q_ref, codes_t, book_ref, book_t, q3, r3, q_t, e_ref, stats_ref, cols,
     pos_col, scale_col, e2, hits, spread, pulled, w3, d_ref,
-    near, far, part_q, half_q, sum_q, up, down, cross,
+    near, far, part_q, half_q, sum_q, ring_in, cross,
     words_b, part_b, half_b, sum_b, first_in, first_sum, second_in, second_sum, last_in,
     sent, arrived, loaded,
 ):
@@ -395,22 +395,6 @@
     q_core.wait_recv()
     sum_q[...] = part_q[rows_at(me.core, half)] + half_q[...]
 
-    z_up, z_down = far_partners[0], far_partners[6]
-
-    def ring_send(step):
-        copies = []
-        for buffers, ahead, steps, device in ((up, 4 - step, 4, z_up), (down, 8 - 3 + step, 3, z_down)):
-            if step >= steps:
-                continue
-            at = rows_at(me.next_z(ahead), chunk)
-            if step == 0:
-                src = sum_q.at[at]
-            else:
-                src = buffers.at[step - 1]
-                src[...] = src[...] + sum_q[at]
-            copies.append(wire.send(src, buffers.at[step], device))
-        return copies
-
     def arrive(copies):
         for copy in copies:
             copy.wait_recv()
@@ -524,47 +508,31 @@
     def q_rows(z):
         return pl.ds(pl.multiple_of(me.core * half + z * chunk, chunk), chunk)
 
-    slices = 3
-    size = chunk // slices
-
-    def q_slice(z, k):
-        return pl.ds(pl.multiple_of(me.core * half + z * chunk + k * size, size), size)
-
     def share(at, device):
         return wire.send(grad_q.at[at], grad_q.at[at], device)
 
-    def pass_on(hop, k):
-        copies = []
-        for back_by, hops, device in ((8 - hop, 4, z_up), (hop, 3, z_down)):
-            if hop < hops:
-                copies.append(share(q_slice(me.next_z(back_by), k), device))
-        return copies
-
     def query_chain():
-        ring = ring_send(0)
-        for step in range(1, 4):
-            yield
-            arrive(ring)
-            ring = ring_send(step)
-        yield
-        arrive(ring)
-        cross[0] = sum_q[rows_at(me.z, chunk)] + (up[3] + down[2])
+        terms = [
+            wire.send(sum_q.at[rows_at(me.next_z(d), chunk)], ring_in.at[d - 1], far_partners[d - 1])
+            for d in (4, 3, 5, 2, 6, 1, 7)
+        ]
+        yield
+        arrive(terms)
+        acc = sum_q[rows_at(me.z, chunk)]
+        for d in range(7):
+            acc = acc + ring_in[d]
+        cross[0] = acc
         across = wire.send(cross.at[0], cross.at[1], partners[1])
         yield
         arrive([across])
         grad_q[q_rows(me.z)] = cross[0] + cross[1]
-        ring = [pass_on(0, k) for k in range(slices)]
         passed.append(share(q_rows(me.z), partners[0]))
-        for hop in range(1, 5):
+        shares = {d: share(q_rows(me.z), far_partners[d - 1]) for d in (4, 3, 5, 2, 6, 1, 7)}
+        for part in ((1, 7, 2), (6, 3, 5, 4)):
             yield
-            following = []
-            for k in range(slices):
-                arrive(ring[k])
-                following.append(pass_on(hop, k) if hop < 4 else [])
-                for ahead, hops in ((8 - hop, 4), (hop, 3)):
-                    if hop - 1 < hops:
-                        passed.append(share(q_slice(me.next_z(ahead), k), partners[0]))
-            ring = following
+            for d in part:
+                arrive([shares[d]])
+                passed.append(share(q_rows(me.next_z(8 - d)), partners[0]))
         yield
 
     large, small = (0, 2 * b_half // 3), (2 * b_half // 3, b_half // 3)
@@ -573,41 +541,35 @@
     gather_words(other, large)
     first = book_chain(large)
     next(first)
-    next(queries)
     gather_words(me.core, large)
     next(first)
-    next(queries)
     gather_words(other, small)
     second = book_chain(small)
     next(second)
     gather_words(me.core, small)
     next(second)
-    next(queries)
     wire.settle()
     next(first)
     next(second)
     wire.settle()
+    next(queries)
     next(first)
+    next(second)
+    wire.settle()
     next(queries)
+    next(first)
     next(second)
-    next(queries)
     wire.settle()
     next(first)
+    next(second)
+    wire.settle()
     next(queries)
+    greet_passed()
+    next(first)
+    next(second)
     wire.settle()
+    next(queries)
     greet_passed()
-    next(second)
-    next(first)
-    next(queries)
-    wire.settle()
-    greet_passed()
-    next(second)
-    next(first)
-    next(queries)
-    wire.settle()
-    greet_passed()
-    next(second)
-    next(queries)
     arrive(passed[taken[0] :])
     wire.finish()
     assert len(wire.copies) == COPIES, len(wire.copies)
@@ -681,8 +643,7 @@
             pltpu.VMEM((rows, width), F32),
             pltpu.VMEM((rows // 2, width), F32),
             pltpu.VMEM((rows // 2, width), F32),
-            pltpu.VMEM((4, chunk, width), F32),
-            pltpu.VMEM((3, chunk, width), F32),
+            pltpu.VMEM((7, chunk, width), F32),
             pltpu.VMEM((2, chunk, width), F32),
             pltpu.VMEM((width, words), F32),
             pltpu.VMEM((words, width), F32),

time: 76.4 us -> 74 us (0.969)
  Pallas kernels: 75.6 us -> 73.2 us
    pallas_call x1, Pallas kernels: 73.2 us -> 70.8 us  [local(): pl.pallas_call(step, in_specs=[hbm, hbm, vmem, hbm], out_specs=(vmem, vme...]
where the time goes in v6:
time: 74 us; the launch traced here: 73.8 us
  Pallas kernels  73.2 us (99%)
    pallas_call x1, Pallas kernels, local(): pl.pallas_call(step, in_specs=[hbm, hbm, vmem, hbm], out_specs=(vmem, vme...  70.8 us
    pallas_call x1, Pallas kernels, local(): pl.pallas_call(hand_over, in_specs=[hbm] * 3, out_specs=[hbm] * 3, out_sh...  2.38 us

profile of v6, /device:TPU:1, one launch (start us, length us, event | category | flops | bytes accessed | tf_op | source)
XLA Modules:
  0.0 73.8 jit_solution(7448521075579057510)
XLA Ops:
  0.6 70.8 %step.1 = (f32[384,768]{1,0:T(8,128)}, f32[256,768]{1,0:T(8,128)}, f32[384]{0:T(512)}) custom-call(f32[384,768]{1,0:T(8,128)} %q_hbm.1, s32[96,1024]{1,0:T(8,128)} %bitcast.1, s32[384]{0:T(512)} %pos_ref.1, f32[256,768]{1,0:T(8,128)} %book_hbm.1), custom_call_target="tpu_custom_call" | custom-call | tf_op jit(solution)/shard_map/step/pallas_call | solution.py:613
  71.5 2.4 %hand_over.1 = (f32[384,768]{1,0:T(8,128)}, f32[256,768]{1,0:T(8,128)}, f32[384]{0:T(512)}) custom-call(f32[384,768]{1,0:T(8,128)} %get-tuple-element.6.refs_0_, f32[256,768]{1,0:T(8,128)} %get-tuple-element.7.refs_1_, f32[384]{0:T(512)} %get-tuple-element.8.refs_2_), custom_call_target="tpu_custom_call" | custom-call | tf_op jit(solution)/shard_map/hand_over/pallas_call | solution.py:666

commit v7 on v6

--- a/solution.py
+++ b/solution.py
@@ -10,7 +10,7 @@
 NT = (((1,), (1,)), ((), ()))
 HIGH_CODES = 64
 LOW_CODES = 4
-COPIES = 114
+COPIES = 130
 
 
 def dot(a, b, dims=NN):
@@ -508,31 +508,42 @@
     def q_rows(z):
         return pl.ds(pl.multiple_of(me.core * half + z * chunk, chunk), chunk)
 
-    def share(at, device):
-        return wire.send(grad_q.at[at], grad_q.at[at], device)
-
     def query_chain():
         terms = [
             wire.send(sum_q.at[rows_at(me.next_z(d), chunk)], ring_in.at[d - 1], far_partners[d - 1])
             for d in (4, 3, 5, 2, 6, 1, 7)
         ]
+        side = lax.rem(me.x, 2)
+        across_width = grad_q.shape[1] // 2
+        ours, theirs = rows_at(side, across_width), rows_at(1 - side, across_width)
+
+        def share(z, columns, device):
+            at = q_rows(z)
+            return wire.send(grad_q.at[at, columns], grad_q.at[at, columns], device)
+
         yield
         arrive(terms)
         acc = sum_q[rows_at(me.z, chunk)]
         for d in range(7):
             acc = acc + ring_in[d]
         cross[0] = acc
-        across = wire.send(cross.at[0], cross.at[1], partners[1])
+        across = wire.send(cross.at[0, :, theirs], cross.at[1, :, theirs], partners[1])
         yield
         arrive([across])
-        grad_q[q_rows(me.z)] = cross[0] + cross[1]
-        passed.append(share(q_rows(me.z), partners[0]))
-        shares = {d: share(q_rows(me.z), far_partners[d - 1]) for d in (4, 3, 5, 2, 6, 1, 7)}
+        grad_q[q_rows(me.z), ours] = cross[0, :, ours] + cross[1, :, ours]
+        shares = {d: share(me.z, ours, far_partners[d - 1]) for d in (4, 3, 5, 2, 6, 1, 7)}
+        beside = {0: share(me.z, ours, partners[1])}
+        passed.append(share(me.z, ours, partners[0]))
         for part in ((1, 7, 2), (6, 3, 5, 4)):
             yield
             for d in part:
                 arrive([shares[d]])
-                passed.append(share(q_rows(me.next_z(8 - d)), partners[0]))
+                beside[d] = share(me.next_z(8 - d), ours, partners[1])
+                passed.append(share(me.next_z(8 - d), ours, partners[0]))
+        yield
+        for d in (0, 1, 7, 2, 6, 3, 5, 4):
+            arrive([beside[d]])
+            passed.append(share(me.next_z(8 - d), theirs, partners[0]))
         yield
 
     large, small = (0, 2 * b_half // 3), (2 * b_half // 3, b_half // 3)
@@ -560,6 +571,8 @@
     next(first)
     next(second)
     wire.settle()
+    next(queries)
+    greet_passed()
     next(first)
     next(second)
     wire.settle()
@@ -570,6 +583,7 @@
     wire.settle()
     next(queries)
     greet_passed()
+    wire.settle()
     arrive(passed[taken[0] :])
     wire.finish()
     assert len(wire.copies) == COPIES, len(wire.copies)

time: 74 us -> 75.6 us (1.022)
  Pallas kernels: 73.2 us -> 74.8 us
    pallas_call x1, Pallas kernels: 70.8 us -> 72.4 us  [local(): pl.pallas_call(step, in_specs=[hbm, hbm, vmem, hbm], out_specs=(vmem, vme...]
where the time goes in v7:
time: 75.6 us; the launch traced here: 75.5 us
  Pallas kernels  74.8 us (99%)
    pallas_call x1, Pallas kernels, local(): pl.pallas_call(step, in_specs=[hbm, hbm, vmem, hbm], out_specs=(vmem, vme...  72.4 us
    pallas_call x1, Pallas kernels, local(): pl.pallas_call(hand_over, in_specs=[hbm] * 3, out_specs=[hbm] * 3, out_sh...  2.38 us

profile of v7, /device:TPU:1, one launch (start us, length us, event | category | flops | bytes accessed | tf_op | source)
XLA Modules:
  0.0 75.5 jit_solution(1533620437390156813)
XLA Ops:
  0.6 72.4 %step.1 = (f32[384,768]{1,0:T(8,128)}, f32[256,768]{1,0:T(8,128)}, f32[384]{0:T(512)}) custom-call(f32[384,768]{1,0:T(8,128)} %q_hbm.1, s32[96,1024]{1,0:T(8,128)} %bitcast.1, s32[384]{0:T(512)} %pos_ref.1, f32[256,768]{1,0:T(8,128)} %book_hbm.1), custom_call_target="tpu_custom_call" | custom-call | tf_op jit(solution)/shard_map/step/pallas_call | solution.py:627
  73.1 2.4 %hand_over.1 = (f32[384,768]{1,0:T(8,128)}, f32[256,768]{1,0:T(8,128)}, f32[384]{0:T(512)}) custom-call(f32[384,768]{1,0:T(8,128)} %get-tuple-element.6.refs_0_, f32[256,768]{1,0:T(8,128)} %get-tuple-element.7.refs_1_, f32[384]{0:T(512)} %get-tuple-element.8.refs_2_), custom_call_target="tpu_custom_call" | custom-call | tf_op jit(solution)/shard_map/hand_over/pallas_call | solution.py:680

commit v8 on v6

--- a/solution.py
+++ b/solution.py
@@ -10,7 +10,7 @@
 NT = (((1,), (1,)), ((), ()))
 HIGH_CODES = 64
 LOW_CODES = 4
-COPIES = 114
+COPIES = 118
 
 
 def dot(a, b, dims=NN):
@@ -331,7 +331,7 @@
     grad_q, grad_b, loss_ref,
     q_ref, codes_t, book_ref, book_t, q3, r3, q_t, e_ref, stats_ref, cols,
     pos_col, scale_col, e2, hits, spread, pulled, w3, d_ref,
-    near, far, part_q, half_q, sum_q, ring_in, cross,
+    near, far, part_q, half_q, sum_q, ring_in, relay, cross,
     words_b, part_b, half_b, sum_b, first_in, first_sum, second_in, second_sum, last_in,
     sent, arrived, loaded,
 ):
@@ -511,11 +511,22 @@
     def share(at, device):
         return wire.send(grad_q.at[at], grad_q.at[at], device)
 
+    middle = grad_q.shape[1] // 2
+
     def query_chain():
         terms = [
             wire.send(sum_q.at[rows_at(me.next_z(d), chunk)], ring_in.at[d - 1], far_partners[d - 1])
-            for d in (4, 3, 5, 2, 6, 1, 7)
+            for d in (3, 5, 2, 6, 1, 7)
         ]
+        sides = ((far_partners[1], slice(0, middle)), (far_partners[5], slice(middle, 2 * middle)))
+        legs = [
+            wire.send(sum_q.at[rows_at(me.next_z(4), chunk), columns], relay.at[k], device)
+            for k, (device, columns) in enumerate(sides)
+        ]
+        yield
+        arrive(legs)
+        for k, (device, columns) in enumerate(sides):
+            terms.append(wire.send(relay.at[k], ring_in.at[3, :, columns], device))
         yield
         arrive(terms)
         acc = sum_q[rows_at(me.z, chunk)]
@@ -527,11 +538,18 @@
         arrive([across])
         grad_q[q_rows(me.z)] = cross[0] + cross[1]
         passed.append(share(q_rows(me.z), partners[0]))
-        shares = {d: share(q_rows(me.z), far_partners[d - 1]) for d in (4, 3, 5, 2, 6, 1, 7)}
-        for part in ((1, 7, 2), (6, 3, 5, 4)):
+        shares = {d: share(q_rows(me.z), far_partners[d - 1]) for d in (2, 6, 3, 5, 1, 7)}
+        yield
+        rest = []
+        for d, (device, columns) in zip((2, 6), sides):
+            at = q_rows(me.next_z(8 - d))
+            arrive([shares[d]])
+            rest.append(wire.send(grad_q.at[at, columns], grad_q.at[at, columns], device))
+            passed.append(share(at, partners[0]))
+        for part in ((1, 7), (3, 5, 4)):
             yield
             for d in part:
-                arrive([shares[d]])
+                arrive(rest if d == 4 else [shares[d]])
                 passed.append(share(q_rows(me.next_z(8 - d)), partners[0]))
         yield
 
@@ -543,6 +561,7 @@
     next(first)
     gather_words(me.core, large)
     next(first)
+    next(queries)
     gather_words(other, small)
     second = book_chain(small)
     next(second)
@@ -560,6 +579,7 @@
     next(first)
     next(second)
     wire.settle()
+    next(queries)
     next(first)
     next(second)
     wire.settle()
@@ -644,6 +664,7 @@
             pltpu.VMEM((rows // 2, width), F32),
             pltpu.VMEM((rows // 2, width), F32),
             pltpu.VMEM((7, chunk, width), F32),
+            pltpu.VMEM((2, chunk, half), F32),
             pltpu.VMEM((2, chunk, width), F32),
             pltpu.VMEM((width, words), F32),
             pltpu.VMEM((words, width), F32),

time: 74 us -> 78.8 us (1.065)
  Pallas kernels: 73.2 us -> 78 us
    pallas_call x1, Pallas kernels: 70.8 us -> 75.6 us  [local(): pl.pallas_call(step, in_specs=[hbm, hbm, vmem, hbm], out_specs=(vmem, vme...]
where the time goes in v8:
time: 78.8 us; the launch traced here: 78.6 us
  Pallas kernels  78 us (99%)
    pallas_call x1, Pallas kernels, local(): pl.pallas_call(step, in_specs=[hbm, hbm, vmem, hbm], out_specs=(vmem, vme...  75.6 us
    pallas_call x1, Pallas kernels, local(): pl.pallas_call(hand_over, in_specs=[hbm] * 3, out_specs=[hbm] * 3, out_sh...  2.38 us

profile of v8, /device:TPU:1, one launch (start us, length us, event | category | flops | bytes accessed | tf_op | source)
XLA Modules:
  0.0 78.6 jit_solution(14121809632114142699)
XLA Ops:
  0.6 75.6 %step.1 = (f32[384,768]{1,0:T(8,128)}, f32[256,768]{1,0:T(8,128)}, f32[384]{0:T(512)}) custom-call(f32[384,768]{1,0:T(8,128)} %q_hbm.1, s32[96,1024]{1,0:T(8,128)} %bitcast.1, s32[384]{0:T(512)} %pos_ref.1, f32[256,768]{1,0:T(8,128)} %book_hbm.1), custom_call_target="tpu_custom_call" | custom-call | tf_op jit(solution)/shard_map/step/pallas_call | solution.py:633
  76.2 2.4 %hand_over.1 = (f32[384,768]{1,0:T(8,128)}, f32[256,768]{1,0:T(8,128)}, f32[384]{0:T(512)}) custom-call(f32[384,768]{1,0:T(8,128)} %get-tuple-element.6.refs_0_, f32[256,768]{1,0:T(8,128)} %get-tuple-element.7.refs_1_, f32[384]{0:T(512)} %get-tuple-element.8.refs_2_), custom_call_target="tpu_custom_call" | custom-call | tf_op jit(solution)/shard_map/hand_over/pallas_call | solution.py:687
